TPU v7x, 1024 devices: a whole 4x8x16 slice. The times are simulated.
1024 devices in a mesh: gx: 32 (over z, core), gy: 4 (over x), gz: 8 (over y).
Axes of the slice: x: 4, y: 8, z: 16, core: 2. Of those that a mesh axis runs over, the one named last changes fastest.
Arguments:
- loads: float32 [128, 655360], P(None, ('gx', 'gy', 'gz')), may hold values from -6 to 6
- stiffness: bfloat16 [655360, 640], P(('gx', 'gy', 'gz')), may hold values from -1 to 3
- stiff_inverse: bfloat16 [655360, 640], P(('gx', 'gy', 'gz')), may hold values from -1 to 1
- face_rows: int32 [1024, 6, 96], P(('gx', 'gy', 'gz')), may hold values from 0 to 639, as said below
- coarse_basis: bfloat16 [196608, 640], P(('gx', 'gy', 'gz')), may hold values from -0.25 to 0.25
- coarse_map: int32 [1024, 192], P(('gx', 'gy', 'gz')), may hold values from 0 to 1535, as said below
- group_rows: bfloat16 [196608, 1536], P(('gx', 'gy', 'gz')), may hold values from -1 to 1, as said below
- root_coupling: bfloat16 [196608, 512], P(('gx', 'gy', 'gz')), may hold values from -1 to 1
- root_inverse: bfloat16 [512, 512], replicated, may hold values from -0.013671875 to 0.013671875
Outputs:
- solution: float32 [128, 655360], P(None, ('gx', 'gy', 'gz'))
- residual: float32 [128, 655360], P(None, ('gx', 'gy', 'gz'))
Inputs may be any that keep to these rules, and one draw needn't show every extreme that they name: `face_rows`: for every subdomain the 6 x 96 entries are distinct; entry i of a face and entry i of the opposite face of the neighbour across it name the same shared dof. `coarse_map`: the 192 entries of a subdomain are distinct. `group_rows`: row i of a subdomain's block is row coarse_map[s, i] of one symmetric matrix of its group; children naming the same group dof hold the same row.
All inputs are finite; a program needn't handle non-finite values.
Results may differ from a plain program's by a relative error of at most 0.014.
Values may be sent and summed in bfloat16 or wider, within the bound.
No kernel may reach another device: no remote copies, remote signals or barrier semaphores. Data moves between devices by JAX's collectives and lax.ppermute only.
A program may use at most 32 MiB of HBM per device.

v0:
```python
import jax
import jax.numpy as jnp
from jax import lax
from jax.sharding import PartitionSpec as P

GROUP_DOFS = 1536


def extended(array, sides, width):
    for axis, dim in sides:
        count, length = (lax.axis_size(axis), array.shape[dim])
        up = [(i, (i + 1) % count) for i in range(count - 1)]
        down = [(j, i) for i, j in up]
        last = lax.slice_in_dim(array, length - width, length, axis=dim)
        first = lax.slice_in_dim(array, 0, width, axis=dim)
        before = lax.ppermute(last, axis, up)
        after = lax.ppermute(first, axis, down)
        array = jnp.concatenate([before, array, after], axis=dim)
    return array


def apply_operator(rounded, stiffness, face_index):
    local_part = jnp.dot(rounded, stiffness, preferred_element_type=jnp.float32)
    face_values = jnp.take(rounded, face_index, axis=1)
    along_x = extended(face_values[:, 0:2], (("gx", 1),), 1)
    along_y = extended(face_values[:, 2:4], (("gy", 1),), 1)
    along_z = extended(face_values[:, 4:6], (("gz", 1),), 1)
    incoming = jnp.stack(
        [along_x[:, 0], along_x[:, 3], along_y[:, 0], along_y[:, 3], along_z[:, 0], along_z[:, 3]],
        axis=1,
    )
    incoming = incoming.reshape(incoming.shape[0], -1).astype(jnp.float32)
    coupled = jnp.zeros(local_part.shape, jnp.float32).at[:, face_index.reshape(-1)].add(incoming)
    return local_part - 0.5 * coupled


def precondition(
    rounded, stiff_inverse, coarse_basis, selector, group_rows, root_coupling, root_inverse
):
    near_part = jnp.dot(rounded, stiff_inverse, preferred_element_type=jnp.float32)
    coarse = lax.dot_general(
        rounded, coarse_basis, (((1,), (1,)), ((), ())), preferred_element_type=jnp.float32
    ).astype(jnp.bfloat16)
    lifted = jnp.dot(coarse, selector, preferred_element_type=jnp.float32)
    root_term = jnp.dot(coarse, root_coupling, preferred_element_type=jnp.float32)
    group_total = lax.psum(lifted, "gx")
    root_total = lax.psum(root_term, ("gx", "gy", "gz"))
    grouped = lax.dot_general(
        group_total.astype(jnp.bfloat16),
        group_rows,
        (((1,), (1,)), ((), ())),
        preferred_element_type=jnp.float32,
    )
    solved = jnp.dot(
        root_total.astype(jnp.bfloat16), root_inverse, preferred_element_type=jnp.float32
    ).astype(jnp.bfloat16)
    from_root = lax.dot_general(
        solved, root_coupling, (((1,), (1,)), ((), ())), preferred_element_type=jnp.float32
    )
    correction = (grouped + from_root).astype(jnp.bfloat16)
    return near_part + jnp.dot(correction, coarse_basis, preferred_element_type=jnp.float32)


def shards(
    loads,
    stiffness,
    stiff_inverse,
    face_rows,
    coarse_basis,
    coarse_map,
    group_rows,
    root_coupling,
    root_inverse,
):
    face_index = face_rows[0]
    selector = (coarse_map[0][:, None] == jnp.arange(GROUP_DOFS, dtype=jnp.int32)[None, :]).astype(
        jnp.bfloat16
    )

    def apply_pre(field):
        return precondition(
            field.astype(jnp.bfloat16),
            stiff_inverse,
            coarse_basis,
            selector,
            group_rows,
            root_coupling,
            root_inverse,
        )

    first = apply_pre(loads)
    after = loads - apply_operator(first.astype(jnp.bfloat16), stiffness, face_index)
    solution = first + apply_pre(after)
    residual = loads - apply_operator(solution.astype(jnp.bfloat16), stiffness, face_index)
    return (solution, residual)


def solution(mesh):
    in_specs = (
        P(None, ("gx", "gy", "gz")),
        P(("gx", "gy", "gz"), None),
        P(("gx", "gy", "gz"), None),
        P(("gx", "gy", "gz"), None, None),
        P(("gx", "gy", "gz"), None),
        P(("gx", "gy", "gz"), None),
        P(("gx", "gy", "gz"), None),
        P(("gx", "gy", "gz"), None),
        P(),
    )
    out_specs = (P(None, ("gx", "gy", "gz")), P(None, ("gx", "gy", "gz")))
    return jax.shard_map(shards, mesh=mesh, in_specs=in_specs, out_specs=out_specs, check_vma=False)
```

profile of v0, /device:TPU:1, one launch (start us, length us, event | category | flops | bytes accessed | tf_op | source)
XLA Modules:
  0.0 521.9 jit_solution(6960282343486071976)
XLA Ops:
  4.6 111.1 %all-reduce.4 = bf16[128,1536]{1,0:T(8,128)(2,1)S(1)} all-reduce(f32[128,1536]{1,0:T(8,128)S(1)} %fusion.4), channel_id=1, replica_groups=mesh['gx'=32,'gy'=4,'gz'=8] {'gx'}, use_global_device_ids=true, to_apply=%region_0.0 | all-reduce | flops 196608 | bytes 1179648 | tf_op jit(solution)/shard_map/psum | solution.py:46
  115.9 124.3 %all-reduce.5 = bf16[128,512]{1,0:T(8,128)(2,1)S(1)} all-reduce(f32[128,512]{1,0:T(8,128)S(1)} %fusion.34), channel_id=1, replica_groups=mesh['gx'=32,'gy'=4,'gz'=8] {'gx','gy','gz'}, use_global_device_ids=true, to_apply=%region_1.0 | all-reduce | flops 65536 | bytes 393216 | tf_op jit(solution)/shard_map/psum | solution.py:47
  243.9 1.9 gather_fusion
  246.0 2.3 collective-permute-start
  248.4 2.1 collective-permute-start.1
  250.5 2.5 collective-permute-start.2
  253.0 1.3 collective-permute-start.3
  255.7 1.3 collective-permute-start.5
  258.0 3.2 collective-permute-done.5
  261.2 6.0 %scatter_custom_fusion = f32[128,640]{0,1:T(8,128)S(1)} fusion(s32[576]{0:T(1024)S(1)} %fusion.29, bf16[128,576]{0,1:T(8,128)(2,1)S(1)} %bitcast.53, f32[]{:T(128)} %constant.1.clone.1), kind=kCustom, calls=%fused_computation.34 | custom fusion | flops 147456 | bytes 475140 | tf_op jit(solution)/shard_map/scatter-add | solution.py:33
  269.8 96.0 %all-reduce.6 = bf16[128,1536]{1,0:T(8,128)(2,1)} all-reduce(f32[128,1536]{1,0:T(8,128)S(1)} %fusion.3), channel_id=1, replica_groups=mesh['gx'=32,'gy'=4,'gz'=8] {'gx'}, use_global_device_ids=true, to_apply=%region_3.5 | all-reduce | flops 196608 | bytes 1179648 | tf_op jit(solution)/shard_map/psum | solution.py:46
  365.7 2.2 fusion.37
  368.0 123.2 %all-reduce.7 = bf16[128,512]{1,0:T(8,128)(2,1)} all-reduce(f32[128,512]{1,0:T(8,128)S(1)} %copy-done.8), channel_id=1, replica_groups=mesh['gx'=32,'gy'=4,'gz'=8] {'gx','gy','gz'}, use_global_device_ids=true, to_apply=%region_4.6 | all-reduce | flops 65536 | bytes 393216 | tf_op jit(solution)/shard_map/psum | solution.py:47
  491.1 1.3 fusion.10
  492.5 1.9 fusion.33
  494.5 1.9 gather_fusion.1
  496.7 3.5 collective-permute-start.6
  500.2 1.9 collective-permute-start.7
  502.1 2.5 collective-permute-start.8
  504.6 1.3 collective-permute-start.9
  505.9 1.9 collective-permute-start.10
  507.9 1.3 collective-permute-start.11
  509.3 5.4 %collective-permute-done.11 = bf16[128,1,96]{0,2,1:T(8,128)(2,1)S(1)} collective-permute-done((bf16[128,1,96]{0,2,1:T(8,128)(2,1)S(1)}, bf16[128,1,96]{0,2,1:T(8,128)(2,1)S(1)}, u32[]{:S(2)}, u32[]{:S(2)}) %collective-permute-start.11) | collective-permute-done | bytes 24608 | tf_op jit(solution)/shard_map/ppermute | solution.py:17
  514.7 6.0 %scatter_custom_fusion.1 = f32[128,640]{0,1:T(8,128)S(1)} fusion(s32[576]{0:T(1024)S(1)} %fusion.29, bf16[128,576]{0,1:T(8,128)(2,1)S(1)} %bitcast.54, f32[]{:T(128)} %constant.1.clone.1), kind=kCustom, calls=%fused_computation.32 | custom fusion | flops 147456 | bytes 475140 | tf_op jit(solution)/shard_map/scatter-add | solution.py:33
  (73 shorter events, 14.3 us)
Async XLA Ops:
  0.6 239.6 %copy-start = (bf16[640,640]{1,0:T(8,128)(2,1)S(1)}, bf16[640,640]{1,0:T(8,128)(2,1)}, u32[]{:S(2)}) copy-start(bf16[640,640]{1,0:T(8,128)(2,1)} %param.13) | copy-start | bytes 2457604
  3.4 112.3 %copy-start.4 = (bf16[192,512]{1,0:T(8,128)(2,1)S(1)}, bf16[192,512]{1,0:T(8,128)(2,1)}, u32[]{:S(2)}) copy-start(bf16[192,512]{1,0:T(8,128)(2,1)} %param.18) | copy-start | bytes 589828
  4.5 235.7 %copy-start.1 = (f32[128,640]{1,0:T(8,128)S(1)}, f32[128,640]{1,0:T(8,128)}, u32[]{:S(2)}) copy-start(f32[128,640]{1,0:T(8,128)} %param.11) | copy-start | bytes 983044
  240.2 1.1 copy-start.5
  241.3 1.0 copy-start.6
  241.3 1.4 copy-start.2
  243.9 11.7 %copy-start.9 = (s32[1,6,96]{2,0,1:T(1,128)S(1)}, s32[1,6,96]{2,0,1:T(1,128)}, u32[]{:S(2)}) copy-start(s32[1,6,96]{2,0,1:T(1,128)} %param.14) | copy-start | bytes 6916
  246.0 21.4 %copy-start.3 = (bf16[640,640]{1,0:T(8,128)(2,1)S(1)}, bf16[640,640]{1,0:T(8,128)(2,1)}, u32[]{:S(2)}) copy-start(bf16[640,640]{1,0:T(8,128)(2,1)} %param.12) | copy-start | bytes 2457604
  246.0 9.7 %collective-permute-start = (bf16[128,1,96]{0,2,1:T(8,128)(2,1)S(1)}, bf16[128,1,96]{0,2,1:T(8,128)(2,1)S(1)}, u32[]{:S(2)}, u32[]{:S(2)}) collective-permute-start(bf16[128,1,96]{0,2,1:T(8,128)(2,1)S(1)} %get-tuple-element.14), channel_id=1, source_target_pairs={{0,32},{32,64},{64,96},{96,128},{128,160},{160,192},{192,224},{224... | collective-permute-start | bytes 73736 | tf_op jit(solution)/shard_map/ppermute | solution.py:16
  248.4 8.7 %collective-permute-start.1 = (bf16[128,1,96]{0,2,1:T(8,128)(2,1)S(1)}, bf16[128,1,96]{0,2,1:T(8,128)(2,1)S(1)}, u32[]{:S(2)}, u32[]{:S(2)}) collective-permute-start(bf16[128,1,96]{0,2,1:T(8,128)(2,1)S(1)} %get-tuple-element.13), channel_id=1, source_target_pairs={{32,0},{64,32},{96,64},{128,96},{160,128},{192,160},{224,192},{256... | collective-permute-start | bytes 73736 | tf_op jit(solution)/shard_map/ppermute | solution.py:17
  250.5 6.5 %collective-permute-start.2 = (bf16[128,1,96]{0,2,1:T(8,128)(2,1)S(1)}, bf16[128,1,96]{0,2,1:T(8,128)(2,1)S(1)}, u32[]{:S(2)}, u32[]{:S(2)}) collective-permute-start(bf16[128,1,96]{0,2,1:T(8,128)(2,1)S(1)} %get-tuple-element.12), channel_id=1, source_target_pairs={{0,8},{8,16},{16,24},{1,9},{9,17},{17,25},{2,10},{10,18},{18,26},{... | collective-permute-start | bytes 73736 | tf_op jit(solution)/shard_map/ppermute | solution.py:16
  253.0 5.0 collective-permute-start.3
  254.3 3.7 collective-permute-start.4
  255.7 5.5 %collective-permute-start.5 = (bf16[128,1,96]{0,2,1:T(8,128)(2,1)S(1)}, bf16[128,1,96]{0,2,1:T(8,128)(2,1)S(1)}, u32[]{:S(2)}, u32[]{:S(2)}) collective-permute-start(bf16[128,1,96]{0,2,1:T(8,128)(2,1)S(1)} %get-tuple-element.9), channel_id=1, source_target_pairs={{1,0},{2,1},{3,2},{4,3},{5,4},{6,5},{7,6},{9,8},{10,9},{11,10},{12... | collective-permute-start | bytes 73736 | tf_op jit(solution)/shard_map/ppermute | solution.py:17
  267.4 0.7 copy-start.10
  365.7 2.2 copy-start.8
  365.7 125.4 %copy-start.7 = (bf16[512,512]{1,0:T(8,128)(2,1)S(1)}, bf16[512,512]{1,0:T(8,128)(2,1)}, u32[]{:S(2)}) copy-start(bf16[512,512]{1,0:T(8,128)(2,1)} %param.19) | copy-start | bytes 1572868
  496.7 11.2 %collective-permute-start.6 = (bf16[128,1,96]{0,2,1:T(8,128)(2,1)S(1)}, bf16[128,1,96]{0,2,1:T(8,128)(2,1)S(1)}, u32[]{:S(2)}, u32[]{:S(2)}) collective-permute-start(bf16[128,1,96]{0,2,1:T(8,128)(2,1)S(1)} %get-tuple-element.8), channel_id=1, source_target_pairs={{0,32},{32,64},{64,96},{96,128},{128,160},{160,192},{192,224},{224... | collective-permute-start | bytes 73736 | tf_op jit(solution)/shard_map/ppermute | solution.py:16
  500.2 9.0 %collective-permute-start.7 = (bf16[128,1,96]{0,2,1:T(8,128)(2,1)S(1)}, bf16[128,1,96]{0,2,1:T(8,128)(2,1)S(1)}, u32[]{:S(2)}, u32[]{:S(2)}) collective-permute-start(bf16[128,1,96]{0,2,1:T(8,128)(2,1)S(1)} %get-tuple-element.7), channel_id=1, source_target_pairs={{32,0},{64,32},{96,64},{128,96},{160,128},{192,160},{224,192},{256... | collective-permute-start | bytes 73736 | tf_op jit(solution)/shard_map/ppermute | solution.py:17
  502.1 7.1 %collective-permute-start.8 = (bf16[128,1,96]{0,2,1:T(8,128)(2,1)S(1)}, bf16[128,1,96]{0,2,1:T(8,128)(2,1)S(1)}, u32[]{:S(2)}, u32[]{:S(2)}) collective-permute-start(bf16[128,1,96]{0,2,1:T(8,128)(2,1)S(1)} %get-tuple-element.6), channel_id=1, source_target_pairs={{0,8},{8,16},{16,24},{1,9},{9,17},{17,25},{2,10},{10,18},{18,26},{... | collective-permute-start | bytes 73736 | tf_op jit(solution)/shard_map/ppermute | solution.py:16
  504.6 4.6 collective-permute-start.9
  505.9 3.3 collective-permute-start.10
  507.9 6.8 %collective-permute-start.11 = (bf16[128,1,96]{0,2,1:T(8,128)(2,1)S(1)}, bf16[128,1,96]{0,2,1:T(8,128)(2,1)S(1)}, u32[]{:S(2)}, u32[]{:S(2)}) collective-permute-start(bf16[128,1,96]{0,2,1:T(8,128)(2,1)S(1)} %get-tuple-element.3), channel_id=1, source_target_pairs={{1,0},{2,1},{3,2},{4,3},{5,4},{6,5},{7,6},{9,8},{10,9},{11,10},{12... | collective-permute-start | bytes 73736 | tf_op jit(solution)/shard_map/ppermute | solution.py:17
where the time goes:
time: 525 us; the launch traced here: 522 us
  blocking collectives  455 us (87%)
  starting transfers between devices  23.3 us (4%)
  other arithmetic  13.8 us (3%)
  matrix products  13.3 us (3%)
  waiting for transfers between devices  9.51 us (2%)
  local copies, waits for them, and re-layouts  6.42 us (1%)
    psum x2, blocking collectives, precondition(): root_total = lax.psum(root_term, ('gx', 'gy', 'gz'))  247 us
    psum x2, blocking collectives, precondition(): group_total = lax.psum(lifted, 'gx')  207 us
    ppermute x6, starting transfers between devices, extended(): before = lax.ppermute(last, axis, up)  14 us
    scatter-add x2, other arithmetic, apply_operator(): jnp.zeros(local_part.shape, jnp.float32).at[:, face_index.reshape(-1)]  12 us
  transfers between devices with their start and end apart: 12, of which 3 were waited for; matrix products, arithmetic and copies ran while one was open for 0% of the time, Pallas kernels for 0%

commit v1 on v0

v1 whole, which is shorter than its diff:
```python
import jax
import jax.numpy as jnp
from jax import lax
from jax.sharding import PartitionSpec as P

GROUP_DOFS = 1536
BF16 = jnp.bfloat16
F32 = jnp.float32
RADIX = 64


def dot(a, b, dims):
    return lax.dot_general(a, b, ((dims[0:1], dims[1:2]), ((), ())), preferred_element_type=F32)


def shift_pairs(count):
    up = [(i, i + 1) for i in range(count - 1)]
    return up, [(j, i) for i, j in up]


def exchange_faces(faces):
    received = []
    for d, axis in enumerate(("gx", "gy", "gz")):
        up, down = shift_pairs(lax.axis_size(axis))
        received.append(lax.ppermute(faces[2 * d + 1], axis, up))
        received.append(lax.ppermute(faces[2 * d], axis, down))
    return received


def high_low(values):
    high = lax.reduce_precision(values, 8, 7)
    return jnp.concatenate([high.astype(BF16), (values - high).astype(BF16)], axis=-2)


def rejoin(rows):
    high, low = jnp.split(rows.astype(F32), 2, axis=-2)
    return high + low


def map_rows(coarse_map):
    padded = jnp.pad(coarse_map[0], (0, 64)).reshape(2, 128)
    digits = jnp.concatenate([padded // RADIX, padded % RADIX], axis=0)
    return jnp.pad(digits, ((0, 12), (0, 0))).astype(BF16)


def shards(
    loads,
    stiffness,
    stiff_inverse,
    face_rows,
    coarse_basis,
    coarse_map,
    group_rows,
    root_coupling,
    root_inverse,
):
    columns = loads.shape[0]
    coarse_dofs, root_dofs = root_coupling.shape
    n_gx, n_gy, n_gz = (lax.axis_size(a) for a in ("gx", "gy", "gz"))
    plane = n_gy * n_gz
    part = columns // plane
    chunks = root_dofs // 128
    same_core = [list(range(c, n_gx, 2)) for c in (0, 1)]
    other_core = [(i, i ^ 1) for i in range(n_gx)]
    flat_faces = face_rows[0].reshape(-1)
    select = (flat_faces[:, None] == jnp.arange(loads.shape[1], dtype=jnp.int32)[None, :]).astype(BF16)
    face_count = face_rows.shape[2]
    digits = map_rows(coarse_map)

    def gathered_map(rows):
        values = rows.astype(F32)
        number = values[:, 0:2] * RADIX + values[:, 2:4]
        return number.reshape(rows.shape[0], -1)[:, :coarse_dofs].reshape(-1).astype(jnp.int32)

    def apply_pre(rounded, selector):
        near = dot(rounded, stiff_inverse, (1, 0))
        coarse_t = dot(coarse_basis, rounded, (1, 1)).astype(BF16)
        root_term = dot(coarse_t, root_coupling, (0, 0)).astype(BF16)
        pieces = lax.all_to_all(
            root_term.reshape(plane, part, root_dofs), ("gy", "gz"), 0, 0, tiled=True
        )
        mine = jnp.sum(pieces.astype(F32), axis=0)
        mine = high_low(mine.reshape(part, chunks, 128).transpose(1, 0, 2).reshape(-1, 128))
        own_rows = mine.shape[0]
        parts = [coarse_t, mine] + ([digits] if selector is None else [])
        payload = jnp.concatenate(parts, axis=0)
        everyone = lax.all_gather(payload, "gx", axis_index_groups=same_core)
        top = coarse_dofs + own_rows
        if selector is None:
            numbers = gathered_map(everyone[:, top : top + 4])
            selector = (
                jnp.arange(GROUP_DOFS, dtype=jnp.int32)[:, None] == numbers[None, :]
            ).astype(BF16)
        group_half = dot(selector, everyone[:, :coarse_dofs].reshape(-1, 128), (1, 0))
        root_half = jnp.sum(rejoin(everyone[:, coarse_dofs:top]), axis=0)
        half = jnp.concatenate([group_half.astype(BF16), high_low(root_half)], axis=0)
        other = lax.ppermute(half, "gx", other_core)
        group_total = (half[:GROUP_DOFS].astype(F32) + other[:GROUP_DOFS].astype(F32)).astype(BF16)
        rows = (root_half + rejoin(other[GROUP_DOFS:])).astype(BF16)
        rows = rows.reshape(chunks, part, 128).transpose(1, 0, 2).reshape(part, root_dofs)
        solved = dot(rows, root_inverse, (1, 0)).astype(BF16)
        solved = lax.all_gather(solved, "gz")
        solved = lax.all_gather(solved, "gy").reshape(columns, root_dofs)
        grouped = dot(group_total, group_rows, (0, 1))
        correction = (grouped + dot(solved, root_coupling, (1, 1))).astype(BF16)
        return near + dot(correction, coarse_basis, (1, 0)), selector

    def operate(rounded):
        faces = dot(select, rounded, (1, 1)).astype(BF16)
        faces = [faces[d * face_count : (d + 1) * face_count] for d in range(6)]
        incoming = exchange_faces(faces)
        local = dot(rounded, stiffness, (1, 0))
        coupled = dot(jnp.concatenate(incoming, axis=0), select, (0, 0))
        return local - 0.5 * coupled

    first, selector = apply_pre(loads.astype(BF16), None)
    after = loads - operate(first.astype(BF16))
    change, _ = apply_pre(after.astype(BF16), selector)
    solution = first + change
    residual = loads - operate(solution.astype(BF16))
    return (solution, residual)


def solution(mesh):
    split = ("gx", "gy", "gz")
    rows = P(split, None)
    in_specs = (P(None, split), rows, rows, P(split, None, None), rows, rows, rows, rows, P())
    out_specs = (P(None, split), P(None, split))
    return jax.shard_map(shards, mesh=mesh, in_specs=in_specs, out_specs=out_specs, check_vma=False)
```

time: 525 us -> 263 us (0.50)
  blocking collectives: 455 us -> 139 us
  starting transfers between devices: 23.3 us -> 78.7 us
  other arithmetic: 13.8 us -> 0.42 us
  matrix products: 13.3 us -> 22.3 us
  waiting for transfers between devices: 9.51 us -> 16.1 us
    psum x4 -> x0, blocking collectives: 455 us -> none  [the longest x2 247 us: precondition(): root_total = lax.psum(root_term, ('gx', 'gy', 'gz'))]
    all_gather x0 -> x6, blocking collectives: none -> 124 us  [the longest x2 68.6 us: apply_pre(): everyone = lax.all_gather(payload, 'gx', axis_index_groups=same_core)]
    ppermute x12 -> x14, starting transfers between devices: 23.3 us -> 68.2 us  [the longest x6 38.8 us: exchange_faces(): received.append(lax.ppermute(faces[2 * d + 1], axis, up))]
    all_to_all x0 -> x1, blocking collectives: none -> 14.3 us  [apply_pre(): lax.all_to_all(root_term.reshape(plane, part, root_dofs), ('gy', 'gz'), 0...]
    scatter-add x2 -> x0, other arithmetic: 12 us -> none  [apply_operator(): jnp.zeros(local_part.shape, jnp.float32).at[:, face_index.reshape(-1)]]
    all_to_all x0 -> x1, starting transfers between devices: none -> 10.5 us  [apply_pre(): lax.all_to_all(root_term.reshape(plane, part, root_dofs), ('gy', 'gz'), 0...]
    all_to_all x0 -> x1, waiting for transfers between devices: none -> 9.1 us  [apply_pre(): lax.all_to_all(root_term.reshape(plane, part, root_dofs), ('gy', 'gz'), 0...]
    dot_general x16 -> x20, matrix products: 13.3 us -> 22.3 us  [dot(): lax.dot_general(a, b, ((dims[0:1], dims[1:2]), ((), ())), preferred_eleme...]
  transfers between devices with their start and end apart: 12 -> 15, of which waited for: 3 -> 6; matrix products, arithmetic and copies ran while one was open for 0% -> 1% of each run, Pallas kernels for 0% -> 0%
where the time goes in v1:
time: 263 us; the launch traced here: 262 us
  blocking collectives  139 us (53%)
  starting transfers between devices  78.7 us (30%)
  matrix products  22.3 us (8%)
  waiting for transfers between devices  16.1 us (6%)
  local copies, waits for them, and re-layouts  4.47 us (2%)
    all_gather x2, blocking collectives, apply_pre(): everyone = lax.all_gather(payload, 'gx', axis_index_groups=same_core)  68.6 us
    ppermute x6, starting transfers between devices, exchange_faces(): received.append(lax.ppermute(faces[2 * d + 1], axis, up))  38.8 us
    all_gather x2, blocking collectives, apply_pre(): solved = lax.all_gather(solved, 'gz')  36.7 us
    dot_general x20, matrix products, dot(): lax.dot_general(a, b, ((dims[0:1], dims[1:2]), ((), ())), preferred_eleme...  22.3 us
    ppermute x2, starting transfers between devices, apply_pre(): other = lax.ppermute(half, 'gx', other_core)  19.3 us
    all_gather x2, blocking collectives, apply_pre(): solved = lax.all_gather(solved, 'gy').reshape(columns, root_dofs)  18.9 us
    all_to_all x1, blocking collectives, apply_pre(): lax.all_to_all(root_term.reshape(plane, part, root_dofs), ('gy', 'gz'), 0...  14.3 us
    all_to_all x1, starting transfers between devices, apply_pre(): lax.all_to_all(root_term.reshape(plane, part, root_dofs), ('gy', 'gz'), 0...  10.5 us
  transfers between devices with their start and end apart: 15, of which 6 were waited for; matrix products, arithmetic and copies ran while one was open for 1% of the time, Pallas kernels for 0%

profile of v1, /device:TPU:1, one launch (start us, length us, event | category | flops | bytes accessed | tf_op | source)
XLA Modules:
  0.0 261.8 jit_solution(4897538941841127324)
XLA Ops:
  3.9 10.5 %all-to-all-start = ((bf16[32,4,512]{2,1,0:T(4,128)(2,1)}), bf16[32,4,512]{2,1,0:T(4,128)(2,1)S(1)}, u32[]{:S(2)}, u32[]{:S(2)}) async-start(bf16[32,4,512]{2,1,0:T(4,128)(2,1)} %reshape.60), calls=%async_computation | async-start | bytes 262144 | tf_op jit(solution)/shard_map/all_to_all | solution.py:79
  14.4 9.1 %all-to-all-done = bf16[32,4,512]{2,1,0:T(4,128)(2,1)S(1)} async-done(((bf16[32,4,512]{2,1,0:T(4,128)(2,1)}), bf16[32,4,512]{2,1,0:T(4,128)(2,1)S(1)}, u32[]{:S(2)}, u32[]{:S(2)}) %all-to-all-start) | async-done | bytes 131104 | tf_op jit(solution)/shard_map/all_to_all | solution.py:79
  23.6 41.7 %all-gather = bf16[3840,128]{1,0:T(8,128)(2,1)S(1)} all-gather(bf16[240,128]{1,0:T(8,128)(2,1)S(1)} %pad_maximum_fusion.2), channel_id=2, replica_groups={{0,64,128,192,256,320,384,448,512,576,640,704,768,832,896,960},{32,96,1..., dimensions={0}, use_global_device_ids=true | all-gather | bytes 1044480 | tf_op jit(solution)/shard_map/all_gather | solution.py:87
  65.6 3.3 %fusion.4 = bf16[1536,128]{1,0:T(8,128)(2,1)S(1)} fusion(bf16[3072,128]{1,0:T(8,128)(2,1)S(1)} %bitcast.87, s32[3072]{0:T(1024)S(1)} %convert_element_type.141), kind=kOutput, calls=%fused_computation.5 | convolution fusion | flops 1212874752 | bytes 1191936 | tf_op jit(solution)/shard_map/dot_general | solution.py:13
  69.8 10.3 %collective-permute-start = (bf16[1568,128]{1,0:T(8,128)(2,1)S(1)}, bf16[1568,128]{1,0:T(8,128)(2,1)S(1)}, u32[]{:S(2)}, u32[]{:S(2)}) collective-permute-start(bf16[1568,128]{1,0:T(8,128)(2,1)S(1)} %pad_maximum_fusion), channel_id=1, source_target_pairs={{0,32},{32,0},{64,96},{96,64},{128,160},{160,128},{192,224},{224,1... | collective-permute-start | bytes 1204232 | tf_op jit(solution)/shard_map/ppermute | solution.py:97
  81.6 18.4 %all-gather.6 = bf16[8,4,512]{2,1,0:T(4,128)(2,1)S(1)} all-gather(bf16[1,4,512]{2,1,0:T(4,128)(2,1)S(1)} %fusion.22), channel_id=3, replica_groups=mesh['gx'=32,'gy'=4,'gz'=8] {'gz'}, dimensions={0}, use_global_device_ids=true | all-gather | bytes 36864 | tf_op jit(solution)/shard_map/all_gather | solution.py:102
  100.1 9.1 %all-gather.2 = bf16[32,4,512]{2,1,0:T(4,128)(2,1)S(1)} all-gather(bf16[8,4,512]{2,1,0:T(4,128)(2,1)S(1)} %all-gather.6), channel_id=4, replica_groups=mesh['gx'=32,'gy'=4,'gz'=8] {'gy'}, dimensions={0}, use_global_device_ids=true | all-gather | bytes 163840 | tf_op jit(solution)/shard_map/all_gather | solution.py:103
  112.9 4.0 %collective-permute-start.5 = (bf16[96,128]{1,0:T(8,128)(2,1)S(1)}, bf16[96,128]{1,0:T(8,128)(2,1)S(1)}, u32[]{:S(2)}, u32[]{:S(2)}) collective-permute-start(bf16[96,128]{1,0:T(8,128)(2,1)S(1)} %get-tuple-element.9), channel_id=1, source_target_pairs={{0,1},{1,2},{2,3},{3,4},{4,5},{5,6},{6,7},{8,9},{9,10},{10,11},{11... | collective-permute-start | bytes 73736 | tf_op jit(solution)/shard_map/ppermute | solution.py:25
  118.2 4.0 %collective-permute-start.3 = (bf16[96,128]{1,0:T(8,128)(2,1)S(1)}, bf16[96,128]{1,0:T(8,128)(2,1)S(1)}, u32[]{:S(2)}, u32[]{:S(2)}) collective-permute-start(bf16[96,128]{1,0:T(8,128)(2,1)S(1)} %get-tuple-element.11), channel_id=1, source_target_pairs={{0,8},{8,16},{16,24},{1,9},{9,17},{17,25},{2,10},{10,18},{18,26},{... | collective-permute-start | bytes 73736 | tf_op jit(solution)/shard_map/ppermute | solution.py:25
  122.2 12.0 %collective-permute-start.1 = (bf16[96,128]{1,0:T(8,128)(2,1)S(1)}, bf16[96,128]{1,0:T(8,128)(2,1)S(1)}, u32[]{:S(2)}, u32[]{:S(2)}) collective-permute-start(bf16[96,128]{1,0:T(8,128)(2,1)S(1)} %get-tuple-element.13), channel_id=1, source_target_pairs={{0,32},{32,64},{64,96},{96,128},{128,160},{160,192},{192,224},{224... | collective-permute-start | bytes 73736 | tf_op jit(solution)/shard_map/ppermute | solution.py:25
  135.2 1.9 collective-permute-start.2
  137.1 3.8 %collective-permute-done.2 = bf16[96,128]{1,0:T(8,128)(2,1)S(1)} collective-permute-done((bf16[96,128]{1,0:T(8,128)(2,1)S(1)}, bf16[96,128]{1,0:T(8,128)(2,1)S(1)}, u32[]{:S(2)}, u32[]{:S(2)}) %collective-permute-start.2) | collective-permute-done | bytes 24608 | tf_op jit(solution)/shard_map/ppermute | solution.py:26
  144.2 14.3 %all_to_all.10 = bf16[32,4,512]{2,1,0:T(4,128)(2,1)S(1)} all-to-all(bf16[32,4,512]{2,1,0:T(4,128)(2,1)} %reshape.69), channel_id=1, replica_groups=mesh['gx'=32,'gy'=4,'gz'=8] {'gy','gz'}, dimensions={0} | all-to-all | bytes 262144 | tf_op jit(solution)/shard_map/all_to_all | solution.py:79
  158.6 26.9 %all-gather.3 = bf16[3584,128]{1,0:T(8,128)(2,1)S(1)} all-gather(bf16[224,128]{1,0:T(8,128)(2,1)S(1)} %pad_maximum_fusion.3), channel_id=5, replica_groups={{0,64,128,192,256,320,384,448,512,576,640,704,768,832,896,960},{32,96,1..., dimensions={0}, use_global_device_ids=true | all-gather | bytes 974848 | tf_op jit(solution)/shard_map/all_gather | solution.py:87
  185.6 3.3 %fusion.5 = bf16[1536,128]{1,0:T(8,128)(2,1)S(1)} fusion(bf16[3072,128]{1,0:T(8,128)(2,1)S(1)} %bitcast.88, s32[3072]{0:T(1024)S(1)} %convert_element_type.141), kind=kOutput, calls=%fused_computation.6 | convolution fusion | flops 1212874752 | bytes 1191936 | tf_op jit(solution)/shard_map/dot_general | solution.py:13
  189.0 9.0 %collective-permute-start.7 = (bf16[1568,128]{1,0:T(8,128)(2,1)S(1)}, bf16[1568,128]{1,0:T(8,128)(2,1)S(1)}, u32[]{:S(2)}, u32[]{:S(2)}) collective-permute-start(bf16[1568,128]{1,0:T(8,128)(2,1)S(1)} %pad_maximum_fusion.1), channel_id=1, source_target_pairs={{0,32},{32,0},{64,96},{96,64},{128,160},{160,128},{192,224},{224,1... | collective-permute-start | bytes 1204232 | tf_op jit(solution)/shard_map/ppermute | solution.py:97
  199.5 18.3 %all-gather.7 = bf16[8,4,512]{2,1,0:T(4,128)(2,1)S(1)} all-gather(bf16[1,4,512]{2,1,0:T(4,128)(2,1)S(1)} %fusion.23), channel_id=6, replica_groups=mesh['gx'=32,'gy'=4,'gz'=8] {'gz'}, dimensions={0}, use_global_device_ids=true | all-gather | bytes 36864 | tf_op jit(solution)/shard_map/all_gather | solution.py:102
  217.8 9.8 %all-gather.5 = bf16[32,4,512]{2,1,0:T(4,128)(2,1)} all-gather(bf16[8,4,512]{2,1,0:T(4,128)(2,1)S(1)} %all-gather.7), channel_id=7, replica_groups=mesh['gx'=32,'gy'=4,'gz'=8] {'gy'}, dimensions={0}, use_global_device_ids=true | all-gather | bytes 163840 | tf_op jit(solution)/shard_map/all_gather | solution.py:103
  229.5 2.6 fusion.12
  233.5 10.8 %collective-permute-start.8 = (bf16[96,128]{1,0:T(8,128)(2,1)S(1)}, bf16[96,128]{1,0:T(8,128)(2,1)S(1)}, u32[]{:S(2)}, u32[]{:S(2)}) collective-permute-start(bf16[96,128]{1,0:T(8,128)(2,1)S(1)} %get-tuple-element.7), channel_id=1, source_target_pairs={{0,32},{32,64},{64,96},{96,128},{128,160},{160,192},{192,224},{224... | collective-permute-start | bytes 73736 | tf_op jit(solution)/shard_map/ppermute | solution.py:25
  246.0 4.0 %collective-permute-start.12 = (bf16[96,128]{1,0:T(8,128)(2,1)S(1)}, bf16[96,128]{1,0:T(8,128)(2,1)S(1)}, u32[]{:S(2)}, u32[]{:S(2)}) collective-permute-start(bf16[96,128]{1,0:T(8,128)(2,1)S(1)} %get-tuple-element.3), channel_id=1, source_target_pairs={{0,1},{1,2},{2,3},{3,4},{4,5},{5,6},{6,7},{8,9},{9,10},{10,11},{11... | collective-permute-start | bytes 73736 | tf_op jit(solution)/shard_map/ppermute | solution.py:25
  251.3 4.0 %collective-permute-start.10 = (bf16[96,128]{1,0:T(8,128)(2,1)S(1)}, bf16[96,128]{1,0:T(8,128)(2,1)S(1)}, u32[]{:S(2)}, u32[]{:S(2)}) collective-permute-start(bf16[96,128]{1,0:T(8,128)(2,1)S(1)} %get-tuple-element.5), channel_id=1, source_target_pairs={{0,8},{8,16},{16,24},{1,9},{9,17},{17,25},{2,10},{10,18},{18,26},{... | collective-permute-start | bytes 73736 | tf_op jit(solution)/shard_map/ppermute | solution.py:25
  255.3 3.1 %collective-permute-start.9 = (bf16[96,128]{1,0:T(8,128)(2,1)S(1)}, bf16[96,128]{1,0:T(8,128)(2,1)S(1)}, u32[]{:S(2)}, u32[]{:S(2)}) collective-permute-start(bf16[96,128]{1,0:T(8,128)(2,1)S(1)} %get-tuple-element.6), channel_id=1, source_target_pairs={{32,0},{64,32},{96,64},{128,96},{160,128},{192,160},{224,192},{256... | collective-permute-start | bytes 73736 | tf_op jit(solution)/shard_map/ppermute | solution.py:26
  258.4 2.0 collective-permute-done.9
  (112 shorter events, 24.3 us)
Async XLA Ops:
  0.6 79.6 %copy-start = (bf16[640,640]{1,0:T(8,128)(2,1)S(1)}, bf16[640,640]{1,0:T(8,128)(2,1)}, u32[]{:S(2)}) copy-start(bf16[640,640]{1,0:T(8,128)(2,1)} %param.11) | copy-start | bytes 2457604
  3.9 19.6 %all-to-all-start = ((bf16[32,4,512]{2,1,0:T(4,128)(2,1)}), bf16[32,4,512]{2,1,0:T(4,128)(2,1)S(1)}, u32[]{:S(2)}, u32[]{:S(2)}) async-start(bf16[32,4,512]{2,1,0:T(4,128)(2,1)} %reshape.60), calls=%async_computation | async-start | bytes 262144 | tf_op jit(solution)/shard_map/all_to_all | solution.py:79
  65.6 14.5 %copy-start.14 = (s32[1,6,96]{2,0,1:T(1,128)S(1)}, s32[1,6,96]{2,0,1:T(1,128)}, u32[]{:S(2)}) copy-start(s32[1,6,96]{2,0,1:T(1,128)} %param.12) | copy-start | bytes 6916
  69.8 11.7 %collective-permute-start = (bf16[1568,128]{1,0:T(8,128)(2,1)S(1)}, bf16[1568,128]{1,0:T(8,128)(2,1)S(1)}, u32[]{:S(2)}, u32[]{:S(2)}) collective-permute-start(bf16[1568,128]{1,0:T(8,128)(2,1)S(1)} %pad_maximum_fusion), channel_id=1, source_target_pairs={{0,32},{32,0},{64,96},{96,64},{128,160},{160,128},{192,224},{224,1... | collective-permute-start | bytes 1204232 | tf_op jit(solution)/shard_map/ppermute | solution.py:97
  80.2 29.0 %copy-start.4 = (bf16[192,512]{1,0:T(8,128)(2,1)S(1)}, bf16[192,512]{1,0:T(8,128)(2,1)}, u32[]{:S(2)}) copy-start(bf16[192,512]{1,0:T(8,128)(2,1)} %param.16) | copy-start | bytes 589828
  81.2 28.2 %copy-start.2 = (bf16[192,640]{1,0:T(8,128)(2,1)S(1)}, bf16[192,640]{1,0:T(8,128)(2,1)}, u32[]{:S(2)}) copy-start(bf16[192,640]{1,0:T(8,128)(2,1)} %param.13) | copy-start | bytes 737284
  81.2 28.2 %copy-start.5 = (bf16[192,1536]{1,0:T(8,128)(2,1)S(1)}, bf16[192,1536]{1,0:T(8,128)(2,1)}, u32[]{:S(2)}) copy-start(bf16[192,1536]{1,0:T(8,128)(2,1)} %param.15) | copy-start | bytes 1769476
  81.4 18.6 %copy-start.12 = (bf16[1568,128]{1,0:T(8,128)(2,1)}, bf16[1568,128]{1,0:T(8,128)(2,1)S(1)}, u32[]{:S(2)}) copy-start(bf16[1568,128]{1,0:T(8,128)(2,1)S(1)} %collective-permute-done) | copy-start | bytes 1204228
  81.6 27.8 %copy-start.10 = (f32[128,640]{1,0:T(8,128)S(1)}, f32[128,640]{1,0:T(8,128)}, u32[]{:S(2)}) copy-start(f32[128,640]{1,0:T(8,128)} %fusion.41) | copy-start | bytes 983044
  111.1 23.1 %copy-start.3 = (bf16[640,640]{1,0:T(8,128)(2,1)S(1)}, bf16[640,640]{1,0:T(8,128)(2,1)}, u32[]{:S(2)}) copy-start(bf16[640,640]{1,0:T(8,128)(2,1)} %param.10) | copy-start | bytes 2457604
  111.6 29.4 %collective-permute-start.6 = (bf16[96,128]{1,0:T(8,128)(2,1)S(1)}, bf16[96,128]{1,0:T(8,128)(2,1)S(1)}, u32[]{:S(2)}, u32[]{:S(2)}) collective-permute-start(bf16[96,128]{1,0:T(8,128)(2,1)S(1)} %get-tuple-element.8), channel_id=1, source_target_pairs={{1,0},{2,1},{3,2},{4,3},{5,4},{6,5},{7,6},{9,8},{10,9},{11,10},{12... | collective-permute-start | bytes 73736 | tf_op jit(solution)/shard_map/ppermute | solution.py:26
  112.9 28.0 %collective-permute-start.5 = (bf16[96,128]{1,0:T(8,128)(2,1)S(1)}, bf16[96,128]{1,0:T(8,128)(2,1)S(1)}, u32[]{:S(2)}, u32[]{:S(2)}) collective-permute-start(bf16[96,128]{1,0:T(8,128)(2,1)S(1)} %get-tuple-element.9), channel_id=1, source_target_pairs={{0,1},{1,2},{2,3},{3,4},{4,5},{5,6},{6,7},{8,9},{9,10},{10,11},{11... | collective-permute-start | bytes 73736 | tf_op jit(solution)/shard_map/ppermute | solution.py:25
  116.9 24.0 %collective-permute-start.4 = (bf16[96,128]{1,0:T(8,128)(2,1)S(1)}, bf16[96,128]{1,0:T(8,128)(2,1)S(1)}, u32[]{:S(2)}, u32[]{:S(2)}) collective-permute-start(bf16[96,128]{1,0:T(8,128)(2,1)S(1)} %get-tuple-element.10), channel_id=1, source_target_pairs={{8,0},{16,8},{24,16},{9,1},{17,9},{25,17},{10,2},{18,10},{26,18},{... | collective-permute-start | bytes 73736 | tf_op jit(solution)/shard_map/ppermute | solution.py:26
  118.2 22.7 %collective-permute-start.3 = (bf16[96,128]{1,0:T(8,128)(2,1)S(1)}, bf16[96,128]{1,0:T(8,128)(2,1)S(1)}, u32[]{:S(2)}, u32[]{:S(2)}) collective-permute-start(bf16[96,128]{1,0:T(8,128)(2,1)S(1)} %get-tuple-element.11), channel_id=1, source_target_pairs={{0,8},{8,16},{16,24},{1,9},{9,17},{17,25},{2,10},{10,18},{18,26},{... | collective-permute-start | bytes 73736 | tf_op jit(solution)/shard_map/ppermute | solution.py:25
  122.2 13.0 %collective-permute-start.1 = (bf16[96,128]{1,0:T(8,128)(2,1)S(1)}, bf16[96,128]{1,0:T(8,128)(2,1)S(1)}, u32[]{:S(2)}, u32[]{:S(2)}) collective-permute-start(bf16[96,128]{1,0:T(8,128)(2,1)S(1)} %get-tuple-element.13), channel_id=1, source_target_pairs={{0,32},{32,64},{64,96},{96,128},{128,160},{160,192},{192,224},{224... | collective-permute-start | bytes 73736 | tf_op jit(solution)/shard_map/ppermute | solution.py:25
  135.2 5.7 %collective-permute-start.2 = (bf16[96,128]{1,0:T(8,128)(2,1)S(1)}, bf16[96,128]{1,0:T(8,128)(2,1)S(1)}, u32[]{:S(2)}, u32[]{:S(2)}) collective-permute-start(bf16[96,128]{1,0:T(8,128)(2,1)S(1)} %get-tuple-element.12), channel_id=1, source_target_pairs={{32,0},{64,32},{96,64},{128,96},{160,128},{192,160},{224,192},{256... | collective-permute-start | bytes 73736 | tf_op jit(solution)/shard_map/ppermute | solution.py:26
  189.0 10.4 %collective-permute-start.7 = (bf16[1568,128]{1,0:T(8,128)(2,1)S(1)}, bf16[1568,128]{1,0:T(8,128)(2,1)S(1)}, u32[]{:S(2)}, u32[]{:S(2)}) collective-permute-start(bf16[1568,128]{1,0:T(8,128)(2,1)S(1)} %pad_maximum_fusion.1), channel_id=1, source_target_pairs={{0,32},{32,0},{64,96},{96,64},{128,160},{160,128},{192,224},{224,1... | collective-permute-start | bytes 1204232 | tf_op jit(solution)/shard_map/ppermute | solution.py:97
  199.3 18.5 %copy-start.13 = (bf16[1568,128]{1,0:T(8,128)(2,1)}, bf16[1568,128]{1,0:T(8,128)(2,1)S(1)}, u32[]{:S(2)}) copy-start(bf16[1568,128]{1,0:T(8,128)(2,1)S(1)} %collective-permute-done.7) | copy-start | bytes 1204228
  233.5 21.7 %collective-permute-start.8 = (bf16[96,128]{1,0:T(8,128)(2,1)S(1)}, bf16[96,128]{1,0:T(8,128)(2,1)S(1)}, u32[]{:S(2)}, u32[]{:S(2)}) collective-permute-start(bf16[96,128]{1,0:T(8,128)(2,1)S(1)} %get-tuple-element.7), channel_id=1, source_target_pairs={{0,32},{32,64},{64,96},{96,128},{128,160},{160,192},{192,224},{224... | collective-permute-start | bytes 73736 | tf_op jit(solution)/shard_map/ppermute | solution.py:25
  244.7 15.8 %collective-permute-start.13 = (bf16[96,128]{1,0:T(8,128)(2,1)S(1)}, bf16[96,128]{1,0:T(8,128)(2,1)S(1)}, u32[]{:S(2)}, u32[]{:S(2)}) collective-permute-start(bf16[96,128]{1,0:T(8,128)(2,1)S(1)} %get-tuple-element.2), channel_id=1, source_target_pairs={{1,0},{2,1},{3,2},{4,3},{5,4},{6,5},{7,6},{9,8},{10,9},{11,10},{12... | collective-permute-start | bytes 73736 | tf_op jit(solution)/shard_map/ppermute | solution.py:26
  246.0 14.5 %collective-permute-start.12 = (bf16[96,128]{1,0:T(8,128)(2,1)S(1)}, bf16[96,128]{1,0:T(8,128)(2,1)S(1)}, u32[]{:S(2)}, u32[]{:S(2)}) collective-permute-start(bf16[96,128]{1,0:T(8,128)(2,1)S(1)} %get-tuple-element.3), channel_id=1, source_target_pairs={{0,1},{1,2},{2,3},{3,4},{4,5},{5,6},{6,7},{8,9},{9,10},{10,11},{11... | collective-permute-start | bytes 73736 | tf_op jit(solution)/shard_map/ppermute | solution.py:25
  250.0 10.5 %collective-permute-start.11 = (bf16[96,128]{1,0:T(8,128)(2,1)S(1)}, bf16[96,128]{1,0:T(8,128)(2,1)S(1)}, u32[]{:S(2)}, u32[]{:S(2)}) collective-permute-start(bf16[96,128]{1,0:T(8,128)(2,1)S(1)} %get-tuple-element.4), channel_id=1, source_target_pairs={{8,0},{16,8},{24,16},{9,1},{17,9},{25,17},{10,2},{18,10},{26,18},{... | collective-permute-start | bytes 73736 | tf_op jit(solution)/shard_map/ppermute | solution.py:26
  251.3 9.2 %collective-permute-start.10 = (bf16[96,128]{1,0:T(8,128)(2,1)S(1)}, bf16[96,128]{1,0:T(8,128)(2,1)S(1)}, u32[]{:S(2)}, u32[]{:S(2)}) collective-permute-start(bf16[96,128]{1,0:T(8,128)(2,1)S(1)} %get-tuple-element.5), channel_id=1, source_target_pairs={{0,8},{8,16},{16,24},{1,9},{9,17},{17,25},{2,10},{10,18},{18,26},{... | collective-permute-start | bytes 73736 | tf_op jit(solution)/shard_map/ppermute | solution.py:25
  255.3 5.1 %collective-permute-start.9 = (bf16[96,128]{1,0:T(8,128)(2,1)S(1)}, bf16[96,128]{1,0:T(8,128)(2,1)S(1)}, u32[]{:S(2)}, u32[]{:S(2)}) collective-permute-start(bf16[96,128]{1,0:T(8,128)(2,1)S(1)} %get-tuple-element.6), channel_id=1, source_target_pairs={{32,0},{64,32},{96,64},{128,96},{160,128},{192,160},{224,192},{256... | collective-permute-start | bytes 73736 | tf_op jit(solution)/shard_map/ppermute | solution.py:26
  (7 other events, 70.2 us)

commit v2 on v1

v2 whole, which is shorter than its diff:
```python
import jax
import jax.numpy as jnp
from jax import lax
from jax.sharding import PartitionSpec as P


GROUP_DOFS = 1536
BF16 = jnp.bfloat16
F32 = jnp.float32
RADIX = 64
PLANE = ("gy", "gz")


def dot(a, b, dims):
    return lax.dot_general(a, b, ((dims[0:1], dims[1:2]), ((), ())), preferred_element_type=F32)


def shift_pairs(count):
    up = [(i, i + 1) for i in range(count - 1)]
    return up, [(j, i) for i, j in up]


def exchange_faces(rows):
    width = rows.shape[0] // 6
    faces = [rows[d * width : (d + 1) * width] for d in range(6)]
    received = []
    for d, axis in enumerate(("gx", "gy", "gz")):
        up, down = shift_pairs(lax.axis_size(axis))
        received.append(lax.ppermute(faces[2 * d + 1], axis, up))
        received.append(lax.ppermute(faces[2 * d], axis, down))
    return jnp.concatenate(received, axis=0)


def high_low(values):
    high = lax.reduce_precision(values, 8, 7)
    return jnp.concatenate([high.astype(BF16), (values - high).astype(BF16)], axis=-2)


def rejoin(rows):
    high, low = jnp.split(rows.astype(F32), 2, axis=-2)
    return high + low


def map_rows(coarse_map):
    padded = jnp.pad(coarse_map[0], (0, 64)).reshape(2, 128)
    digits = jnp.concatenate([padded // RADIX, padded % RADIX], axis=0)
    return jnp.pad(digits, ((0, 12), (0, 0))).astype(BF16)


def shards(
    loads,
    stiffness,
    stiff_inverse,
    face_rows,
    coarse_basis,
    coarse_map,
    group_rows,
    root_coupling,
    root_inverse,
):
    coarse_dofs, root_dofs = root_coupling.shape
    n_gx, n_gy, n_gz = (lax.axis_size(a) for a in ("gx", "gy", "gz"))
    plane = n_gy * n_gz
    part = root_dofs // plane
    same_core = [list(range(c, n_gx, 2)) for c in (0, 1)]
    other_core = [(i, i ^ 1) for i in range(n_gx)]
    flat_faces = face_rows[0].reshape(-1)
    select = (flat_faces[:, None] == jnp.arange(loads.shape[1], dtype=jnp.int32)[None, :]).astype(BF16)
    digits = map_rows(coarse_map)
    basis_faces = dot(select, coarse_basis, (1, 1)).astype(BF16)
    root_at_faces = dot(basis_faces, root_coupling, (1, 0)).astype(BF16)

    def gathered_map(rows):
        values = rows.astype(F32)
        number = values[:, 0:2] * RADIX + values[:, 2:4]
        return number.reshape(rows.shape[0], -1)[:, :coarse_dofs].reshape(-1).astype(jnp.int32)

    def apply_pre(rounded, selector):
        near = dot(rounded, stiff_inverse, (1, 0))
        coarse_t = dot(coarse_basis, rounded, (1, 1)).astype(BF16)
        root_term = dot(root_coupling, coarse_t, (0, 0)).astype(BF16)
        pieces = lax.all_to_all(root_term.reshape(plane, part, 128), PLANE, 0, 0, tiled=True)
        parts = [coarse_t] + ([digits] if selector is None else [])
        everyone = lax.all_gather(jnp.concatenate(parts, axis=0), "gx", axis_index_groups=same_core)
        mine = jnp.sum(pieces.astype(F32), axis=0)
        pair = mine + rejoin(lax.ppermute(high_low(mine), "gx", other_core))
        spread = jnp.broadcast_to(high_low(pair)[None], (n_gx // 2, 2 * part, 128))
        lines = lax.all_to_all(spread, "gx", 0, 0, axis_index_groups=same_core, tiled=True)
        root_rows = jnp.sum(rejoin(lines), axis=0)
        spread = jnp.broadcast_to(root_rows.astype(BF16)[None], (plane, part, 128))
        root_total = lax.all_to_all(spread, PLANE, 0, 0, tiled=True).reshape(root_dofs, 128)
        if selector is None:
            numbers = gathered_map(everyone[:, coarse_dofs : coarse_dofs + 4])
            selector = (
                jnp.arange(GROUP_DOFS, dtype=jnp.int32)[:, None] == numbers[None, :]
            ).astype(BF16)
        group_half = dot(selector, everyone[:, :coarse_dofs].reshape(-1, 128), (1, 0)).astype(BF16)
        group_half = lax.optimization_barrier(group_half)
        other = lax.ppermute(group_half, "gx", other_core)
        group_total = (group_half.astype(F32) + other.astype(F32)).astype(BF16)
        grouped = dot(group_rows, group_total, (1, 0)).astype(BF16)
        grouped = lax.optimization_barrier(grouped)
        without_root = near + dot(grouped, coarse_basis, (0, 0))
        solved = dot(root_inverse, root_total, (0, 0)).astype(BF16)
        from_root = dot(root_coupling, solved, (1, 0)).astype(BF16)
        return without_root, dot(from_root, coarse_basis, (0, 0)), solved, selector

    def operate(without_root, total, solved, root_at_neighbours):
        faces = dot(select, without_root.astype(BF16), (1, 1)).astype(BF16)
        if root_at_neighbours is None:
            received = exchange_faces(jnp.concatenate([faces, root_at_faces], axis=1))
            incoming, root_at_neighbours = received[:, :128], received[:, 128:]
        else:
            incoming = exchange_faces(faces)
        coupled = lax.optimization_barrier(dot(incoming, select, (0, 0)))
        at_faces = dot(root_at_neighbours, solved, (1, 0)).astype(BF16)
        local = dot(total.astype(BF16), stiffness, (1, 0))
        return local - 0.5 * (coupled + dot(at_faces, select, (0, 0))), root_at_neighbours

    base, root_part, solved, selector = apply_pre(loads.astype(BF16), None)
    first = base + root_part
    applied, root_at_neighbours = operate(base, first, solved, None)
    after = loads - applied
    change, root_change, solved_change, _ = apply_pre(after.astype(BF16), selector)
    base = base + change
    solved_sum = solved.astype(F32) + solved_change.astype(F32)
    solution = first + (change + root_change)
    applied, _ = operate(base, solution, solved_sum.astype(BF16), root_at_neighbours)
    residual = loads - applied
    return (solution, residual)


def solution(mesh):
    split = ("gx", "gy", "gz")
    rows = P(split, None)
    in_specs = (P(None, split), rows, rows, P(split, None, None), rows, rows, rows, rows, P())
    out_specs = (P(None, split), P(None, split))
    return jax.shard_map(shards, mesh=mesh, in_specs=in_specs, out_specs=out_specs, check_vma=False)
```

time: 263 us -> 243 us (0.924)
  blocking collectives: 139 us -> 68.9 us
  starting transfers between devices: 78.7 us -> 101 us
  matrix products: 22.3 us -> 32.4 us
  local copies, waits for them, and re-layouts: 4.47 us -> 13.4 us
  waiting for transfers between devices: 16.1 us -> 23.2 us
    all_gather x6 -> x2, blocking collectives: 124 us -> 68.9 us  [apply_pre(): lax.all_gather(jnp.concatenate(parts, axis=0), 'gx', axis_index_groups=sa...]
    all_to_all x1 -> x6, starting transfers between devices: 10.5 us -> 46.3 us  [the longest x2 18.3 us: apply_pre(): lax.all_to_all(spread, PLANE, 0, 0, tiled=True).reshape(root_dofs, 128)]
    ppermute x6, starting transfers between devices: 38.8 us -> 16.4 us  [exchange_faces(): received.append(lax.ppermute(faces[2 * d + 1], axis, up))]
    all_to_all x1 -> x0, blocking collectives: 14.3 us -> none  [apply_pre(): lax.all_to_all(root_term.reshape(plane, part, root_dofs), ('gy', 'gz'), 0...]
    all_to_all x1 -> x6, waiting for transfers between devices: 9.1 us -> 22.3 us  [the longest x2 12.7 us: apply_pre(): lax.all_to_all(spread, PLANE, 0, 0, tiled=True).reshape(root_dofs, 128)]
    dot_general x20 -> x25, matrix products: 22.3 us -> 32.4 us  [dot(): lax.dot_general(a, b, ((dims[0:1], dims[1:2]), ((), ())), preferred_eleme...]
    ppermute x2 -> x4, starting transfers between devices: 19.3 us -> 28.5 us  [the longest x2 22.4 us: apply_pre(): other = lax.ppermute(group_half, 'gx', other_core)]
    unnamed x43 -> x33, local copies, waits for them, and re-layouts: 0.87 us -> 7.7 us
  transfers between devices with their start and end apart: 15 -> 22, of which waited for: 6 -> 5; matrix products, arithmetic and copies ran while one was open for 1% -> 9% of each run, Pallas kernels for 0% -> 0%
where the time goes in v2:
time: 243 us; the launch traced here: 241 us
  starting transfers between devices  101 us (42%)
  blocking collectives  68.9 us (28%)
  matrix products  32.4 us (13%)
  waiting for transfers between devices  23.2 us (10%)
  local copies, waits for them, and re-layouts  13.4 us (6%)
    all_gather x2, blocking collectives, apply_pre(): lax.all_gather(jnp.concatenate(parts, axis=0), 'gx', axis_index_groups=sa...  68.9 us
    dot_general x25, matrix products, dot(): lax.dot_general(a, b, ((dims[0:1], dims[1:2]), ((), ())), preferred_eleme...  32.4 us
    ppermute x2, starting transfers between devices, apply_pre(): other = lax.ppermute(group_half, 'gx', other_core)  22.4 us
    all_to_all x2, starting transfers between devices, apply_pre(): lax.all_to_all(spread, PLANE, 0, 0, tiled=True).reshape(root_dofs, 128)  18.3 us
    ppermute x6, starting transfers between devices, exchange_faces(): received.append(lax.ppermute(faces[2 * d + 1], axis, up))  16.4 us
    all_to_all x2, starting transfers between devices, apply_pre(): lax.all_to_all(spread, 'gx', 0, 0, axis_index_groups=same_core, tiled=True)  14.5 us
    all_to_all x2, starting transfers between devices, apply_pre(): lax.all_to_all(root_term.reshape(plane, part, 128), PLANE, 0, 0, tiled=True)  13.5 us
    all_to_all x2, waiting for transfers between devices, apply_pre(): lax.all_to_all(spread, PLANE, 0, 0, tiled=True).reshape(root_dofs, 128)  12.7 us
  transfers between devices with their start and end apart: 22, of which 5 were waited for; matrix products, arithmetic and copies ran while one was open for 9% of the time, Pallas kernels for 0%

profile of v2, /device:TPU:1, one launch (start us, length us, event | category | flops | bytes accessed | tf_op | source)
XLA Modules:
  0.0 241.2 jit_solution(7437125909250589631)
XLA Ops:
  2.8 41.0 %all-gather = bf16[3328,128]{1,0:T(8,128)(2,1)S(1)} all-gather(bf16[208,128]{1,0:T(8,128)(2,1)S(1)} %pad_maximum_fusion.1), channel_id=2, replica_groups={{0,64,128,192,256,320,384,448,512,576,640,704,768,832,896,960},{32,96,1..., dimensions={0}, use_global_device_ids=true | all-gather | bytes 905216 | tf_op jit(solution)/shard_map/all_gather | solution.py:84
  44.0 4.1 %fusion.4 = bf16[1536,128]{1,0:T(8,128)(2,1)} fusion(bf16[3072,128]{1,0:T(8,128)(2,1)S(1)} %bitcast.76, s32[3072]{0:T(1024)S(1)} %convert_element_type.197), kind=kOutput, calls=%fused_computation.5 | convolution fusion | flops 1212874752 | bytes 1191936 | tf_op jit(solution)/shard_map/dot_general | solution.py:15
  48.1 9.8 %collective-permute-start = (bf16[1536,128]{1,0:T(8,128)(2,1)}, bf16[1536,128]{1,0:T(8,128)(2,1)}, u32[]{:S(2)}, u32[]{:S(2)}) collective-permute-start(bf16[1536,128]{1,0:T(8,128)(2,1)} %fusion.4), channel_id=1, source_target_pairs={{0,32},{32,0},{64,96},{96,64},{128,160},{160,128},{192,224},{224,1... | collective-permute-start | bytes 1179656 | tf_op jit(solution)/shard_map/ppermute | solution.py:99
  58.9 9.7 %all-to-all-start = ((bf16[32,16,128]{2,1,0:T(8,128)(2,1)}), bf16[32,16,128]{2,1,0:T(8,128)(2,1)S(1)}, u32[]{:S(2)}, u32[]{:S(2)}) async-start(bf16[32,16,128]{2,1,0:T(8,128)(2,1)} %bitcast.6), calls=%async_computation | async-start | bytes 262144 | tf_op jit(solution)/shard_map/all_to_all | solution.py:82
  69.1 8.7 %all-to-all-done = bf16[32,16,128]{2,1,0:T(8,128)(2,1)S(1)} async-done(((bf16[32,16,128]{2,1,0:T(8,128)(2,1)}), bf16[32,16,128]{2,1,0:T(8,128)(2,1)S(1)}, u32[]{:S(2)}, u32[]{:S(2)}) %all-to-all-start) | async-done | bytes 131104 | tf_op jit(solution)/shard_map/all_to_all | solution.py:82
  77.8 4.1 %collective-permute-start.1 = (bf16[32,128]{1,0:T(8,128)(2,1)S(1)}, bf16[32,128]{1,0:T(8,128)(2,1)S(1)}, u32[]{:S(2)}, u32[]{:S(2)}) collective-permute-start(bf16[32,128]{1,0:T(8,128)(2,1)S(1)} %pad_maximum_fusion.2), channel_id=1, source_target_pairs={{0,32},{32,0},{64,96},{96,64},{128,160},{160,128},{192,224},{224,1... | collective-permute-start | bytes 24584 | tf_op jit(solution)/shard_map/ppermute | solution.py:86
  87.0 2.4 collective-permute-start.3
  90.1 4.9 %all-to-all-start.1 = ((bf16[16,32,128]{2,1,0:T(8,128)(2,1)}), bf16[16,32,128]{2,1,0:T(8,128)(2,1)S(1)}, u32[]{:S(2)}, u32[]{:S(2)}) async-start(bf16[16,32,128]{2,1,0:T(8,128)(2,1)} %broadcast_in_dim.8), calls=%async_computation.1 | async-start | bytes 262144 | tf_op jit(solution)/shard_map/all_to_all | solution.py:88
  95.0 2.2 collective-permute-start.4
  98.5 2.9 %collective-permute-start.6 = (bf16[96,640]{1,0:T(8,128)(2,1)S(1)}, bf16[96,640]{1,0:T(8,128)(2,1)S(1)}, u32[]{:S(2)}, u32[]{:S(2)}) collective-permute-start(bf16[96,640]{1,0:T(8,128)(2,1)S(1)} %get-tuple-element.7), channel_id=1, source_target_pairs={{0,1},{1,2},{2,3},{3,4},{4,5},{5,6},{6,7},{8,9},{9,10},{10,11},{11... | collective-permute-start | bytes 368648 | tf_op jit(solution)/shard_map/ppermute | solution.py:29
  107.7 6.6 %all-to-all-start.2 = ((bf16[32,16,128]{2,1,0:T(8,128)(2,1)}), bf16[32,16,128]{2,1,0:T(8,128)(2,1)S(1)}, u32[]{:S(2)}, u32[]{:S(2)}) async-start(bf16[32,16,128]{2,1,0:T(8,128)(2,1)} %broadcast_in_dim.9), calls=%async_computation.2 | async-start | bytes 262144 | tf_op jit(solution)/shard_map/all_to_all | solution.py:91
  117.1 6.3 %all-to-all-done.2 = bf16[32,16,128]{2,1,0:T(8,128)(2,1)S(1)} async-done(((bf16[32,16,128]{2,1,0:T(8,128)(2,1)}), bf16[32,16,128]{2,1,0:T(8,128)(2,1)S(1)}, u32[]{:S(2)}, u32[]{:S(2)}) %all-to-all-start.2) | async-done | bytes 131104 | tf_op jit(solution)/shard_map/all_to_all | solution.py:91
  123.7 2.6 %fusion.9 = f32[128,640]{1,0:T(8,128)} fusion(bf16[128,512]{1,0:T(8,128)(2,1)S(1)} %convolution_convert_fusion.4, s32[576]{0:T(1024)S(1)} %eq.33, bf16[576,640]{1,0:T(8,128)(2,1)} %constant_dynamic-update-slice_fusion), kind=kOutput, calls=%fused_computation.16 | convolution fusion | flops 170311680 | bytes 1050880 | tf_op jit(solution)/shard_map/dot_general | solution.py:15
  130.1 3.9 %all-to-all-start.3 = ((bf16[32,16,128]{2,1,0:T(8,128)(2,1)}), bf16[32,16,128]{2,1,0:T(8,128)(2,1)S(1)}, u32[]{:S(2)}, u32[]{:S(2)}) async-start(bf16[32,16,128]{2,1,0:T(8,128)(2,1)} %bitcast.77), calls=%async_computation.3 | async-start | bytes 262144 | tf_op jit(solution)/shard_map/all_to_all | solution.py:82
  134.0 27.9 %all-gather.1 = bf16[3072,128]{1,0:T(8,128)(2,1)S(1)} all-gather(bf16[192,128]{1,0:T(8,128)(2,1)S(1)} %bitcast.80), channel_id=3, replica_groups={{0,64,128,192,256,320,384,448,512,576,640,704,768,832,896,960},{32,96,1..., dimensions={0}, use_global_device_ids=true | all-gather | bytes 835584 | tf_op jit(solution)/shard_map/all_gather | solution.py:84
  161.8 4.1 %fusion.5 = bf16[1536,128]{1,0:T(8,128)(2,1)} fusion(bf16[3072,128]{1,0:T(8,128)(2,1)S(1)} %all-gather.1, s32[3072]{0:T(1024)S(1)} %convert_element_type.197), kind=kOutput, calls=%fused_computation.6 | convolution fusion | flops 1212874752 | bytes 1191936 | tf_op jit(solution)/shard_map/dot_general | solution.py:15
  166.0 12.6 %collective-permute-start.8 = (bf16[1536,128]{1,0:T(8,128)(2,1)}, bf16[1536,128]{1,0:T(8,128)(2,1)}, u32[]{:S(2)}, u32[]{:S(2)}) collective-permute-start(bf16[1536,128]{1,0:T(8,128)(2,1)} %fusion.5), channel_id=1, source_target_pairs={{0,32},{32,0},{64,96},{96,64},{128,160},{160,128},{192,224},{224,1... | collective-permute-start | bytes 1179656 | tf_op jit(solution)/shard_map/ppermute | solution.py:99
  184.0 2.3 collective-permute-start.10
  187.1 9.6 %all-to-all-start.4 = ((bf16[16,32,128]{2,1,0:T(8,128)(2,1)}), bf16[16,32,128]{2,1,0:T(8,128)(2,1)S(1)}, u32[]{:S(2)}, u32[]{:S(2)}) async-start(bf16[16,32,128]{2,1,0:T(8,128)(2,1)} %broadcast_in_dim.10), calls=%async_computation.4 | async-start | bytes 262144 | tf_op jit(solution)/shard_map/all_to_all | solution.py:88
  198.6 3.9 %collective-permute-start.12 = (bf16[96,128]{1,0:T(8,128)(2,1)S(1)}, bf16[96,128]{1,0:T(8,128)(2,1)S(1)}, u32[]{:S(2)}, u32[]{:S(2)}) collective-permute-start(bf16[96,128]{1,0:T(8,128)(2,1)S(1)} %get-tuple-element.11), channel_id=1, source_target_pairs={{0,8},{8,16},{16,24},{1,9},{9,17},{17,25},{2,10},{10,18},{18,26},{... | collective-permute-start | bytes 73736 | tf_op jit(solution)/shard_map/ppermute | solution.py:29
  203.8 3.1 %collective-permute-start.14 = (bf16[96,128]{1,0:T(8,128)(2,1)S(1)}, bf16[96,128]{1,0:T(8,128)(2,1)S(1)}, u32[]{:S(2)}, u32[]{:S(2)}) collective-permute-start(bf16[96,128]{1,0:T(8,128)(2,1)S(1)} %get-tuple-element.9), channel_id=1, source_target_pairs={{0,1},{1,2},{2,3},{3,4},{4,5},{5,6},{6,7},{8,9},{9,10},{10,11},{11... | collective-permute-start | bytes 73736 | tf_op jit(solution)/shard_map/ppermute | solution.py:29
  212.0 11.7 %all-to-all-start.5 = ((bf16[32,16,128]{2,1,0:T(8,128)(2,1)}), bf16[32,16,128]{2,1,0:T(8,128)(2,1)S(1)}, u32[]{:S(2)}, u32[]{:S(2)}) async-start(bf16[32,16,128]{2,1,0:T(8,128)(2,1)} %broadcast_in_dim.11), calls=%async_computation.5 | async-start | bytes 262144 | tf_op jit(solution)/shard_map/all_to_all | solution.py:91
  226.5 6.4 %all-to-all-done.5 = bf16[32,16,128]{2,1,0:T(8,128)(2,1)S(1)} async-done(((bf16[32,16,128]{2,1,0:T(8,128)(2,1)}), bf16[32,16,128]{2,1,0:T(8,128)(2,1)S(1)}, u32[]{:S(2)}, u32[]{:S(2)}) %all-to-all-start.5) | async-done | bytes 131104 | tf_op jit(solution)/shard_map/all_to_all | solution.py:91
  234.9 2.6 %fusion.6 = f32[128,640]{1,0:T(8,128)} fusion(s32[576]{0:T(1024)S(1)} %eq.33, bf16[576,640]{1,0:T(8,128)(2,1)} %constant_dynamic-update-slice_fusion, bf16[128,512]{1,0:T(8,128)(2,1)S(1)} %convolution_convert_fusion.3, bf16[128,512]{1,0:T(8,128)(2,1)S(1)} %convolution_convert_fusion.4), kind=kOutput, calls=%fused_computation.13 | convolution fusion | flops 170573824 | bytes 1181952 | tf_op jit(solution)/shard_map/dot_general | solution.py:15
  (116 shorter events, 46.3 us)
Async XLA Ops:
  0.6 68.1 %copy-start = (bf16[640,640]{1,0:T(8,128)(2,1)S(1)}, bf16[640,640]{1,0:T(8,128)(2,1)}, u32[]{:S(2)}) copy-start(bf16[640,640]{1,0:T(8,128)(2,1)} %param.11) | copy-start | bytes 2457604
  48.1 20.6 %copy-start.2 = (f32[128,640]{1,0:T(8,128)S(1)}, f32[128,640]{1,0:T(8,128)}, u32[]{:S(2)}) copy-start(f32[128,640]{1,0:T(8,128)} %param.9) | copy-start | bytes 983044
  48.1 34.7 %collective-permute-start = (bf16[1536,128]{1,0:T(8,128)(2,1)}, bf16[1536,128]{1,0:T(8,128)(2,1)}, u32[]{:S(2)}, u32[]{:S(2)}) collective-permute-start(bf16[1536,128]{1,0:T(8,128)(2,1)} %fusion.4), channel_id=1, source_target_pairs={{0,32},{32,0},{64,96},{96,64},{128,160},{160,128},{192,224},{224,1... | collective-permute-start | bytes 1179656 | tf_op jit(solution)/shard_map/ppermute | solution.py:99
  58.9 18.8 %all-to-all-start = ((bf16[32,16,128]{2,1,0:T(8,128)(2,1)}), bf16[32,16,128]{2,1,0:T(8,128)(2,1)S(1)}, u32[]{:S(2)}, u32[]{:S(2)}) async-start(bf16[32,16,128]{2,1,0:T(8,128)(2,1)} %bitcast.6), calls=%async_computation | async-start | bytes 262144 | tf_op jit(solution)/shard_map/all_to_all | solution.py:82
  77.8 4.9 %collective-permute-start.1 = (bf16[32,128]{1,0:T(8,128)(2,1)S(1)}, bf16[32,128]{1,0:T(8,128)(2,1)S(1)}, u32[]{:S(2)}, u32[]{:S(2)}) collective-permute-start(bf16[32,128]{1,0:T(8,128)(2,1)S(1)} %pad_maximum_fusion.2), channel_id=1, source_target_pairs={{0,32},{32,0},{64,96},{96,64},{128,160},{160,128},{192,224},{224,1... | collective-permute-start | bytes 24584 | tf_op jit(solution)/shard_map/ppermute | solution.py:86
  85.0 16.4 %collective-permute-start.2 = (bf16[96,640]{1,0:T(8,128)(2,1)S(1)}, bf16[96,640]{1,0:T(8,128)(2,1)S(1)}, u32[]{:S(2)}, u32[]{:S(2)}) collective-permute-start(bf16[96,640]{1,0:T(8,128)(2,1)S(1)} %get-tuple-element.3), channel_id=1, source_target_pairs={{0,32},{32,64},{64,96},{96,128},{128,160},{160,192},{192,224},{224... | collective-permute-start | bytes 368648 | tf_op jit(solution)/shard_map/ppermute | solution.py:29
  87.0 16.5 %collective-permute-start.3 = (bf16[96,640]{1,0:T(8,128)(2,1)S(1)}, bf16[96,640]{1,0:T(8,128)(2,1)S(1)}, u32[]{:S(2)}, u32[]{:S(2)}) collective-permute-start(bf16[96,640]{1,0:T(8,128)(2,1)S(1)} %get-tuple-element.4), channel_id=1, source_target_pairs={{32,0},{64,32},{96,64},{128,96},{160,128},{192,160},{224,192},{256... | collective-permute-start | bytes 368648 | tf_op jit(solution)/shard_map/ppermute | solution.py:30
  90.1 16.9 %all-to-all-start.1 = ((bf16[16,32,128]{2,1,0:T(8,128)(2,1)}), bf16[16,32,128]{2,1,0:T(8,128)(2,1)S(1)}, u32[]{:S(2)}, u32[]{:S(2)}) async-start(bf16[16,32,128]{2,1,0:T(8,128)(2,1)} %broadcast_in_dim.8), calls=%async_computation.1 | async-start | bytes 262144 | tf_op jit(solution)/shard_map/all_to_all | solution.py:88
  95.0 9.1 %collective-permute-start.4 = (bf16[96,640]{1,0:T(8,128)(2,1)S(1)}, bf16[96,640]{1,0:T(8,128)(2,1)S(1)}, u32[]{:S(2)}, u32[]{:S(2)}) collective-permute-start(bf16[96,640]{1,0:T(8,128)(2,1)S(1)} %get-tuple-element.5), channel_id=1, source_target_pairs={{0,8},{8,16},{16,24},{1,9},{9,17},{17,25},{2,10},{10,18},{18,26},{... | collective-permute-start | bytes 368648 | tf_op jit(solution)/shard_map/ppermute | solution.py:29
  97.2 7.5 %collective-permute-start.5 = (bf16[96,640]{1,0:T(8,128)(2,1)S(1)}, bf16[96,640]{1,0:T(8,128)(2,1)S(1)}, u32[]{:S(2)}, u32[]{:S(2)}) collective-permute-start(bf16[96,640]{1,0:T(8,128)(2,1)S(1)} %get-tuple-element.6), channel_id=1, source_target_pairs={{8,0},{16,8},{24,16},{9,1},{17,9},{25,17},{10,2},{18,10},{26,18},{... | collective-permute-start | bytes 368648 | tf_op jit(solution)/shard_map/ppermute | solution.py:30
  98.5 6.9 %collective-permute-start.6 = (bf16[96,640]{1,0:T(8,128)(2,1)S(1)}, bf16[96,640]{1,0:T(8,128)(2,1)S(1)}, u32[]{:S(2)}, u32[]{:S(2)}) collective-permute-start(bf16[96,640]{1,0:T(8,128)(2,1)S(1)} %get-tuple-element.7), channel_id=1, source_target_pairs={{0,1},{1,2},{2,3},{3,4},{4,5},{5,6},{6,7},{8,9},{9,10},{10,11},{11... | collective-permute-start | bytes 368648 | tf_op jit(solution)/shard_map/ppermute | solution.py:29
  101.5 12.9 %collective-permute-start.7 = (bf16[96,640]{1,0:T(8,128)(2,1)S(1)}, bf16[96,640]{1,0:T(8,128)(2,1)S(1)}, u32[]{:S(2)}, u32[]{:S(2)}) collective-permute-start(bf16[96,640]{1,0:T(8,128)(2,1)S(1)} %get-tuple-element.2), channel_id=1, source_target_pairs={{1,0},{2,1},{3,2},{4,3},{5,4},{6,5},{7,6},{9,8},{10,9},{11,10},{12... | collective-permute-start | bytes 368648 | tf_op jit(solution)/shard_map/ppermute | solution.py:30
  107.7 15.7 %all-to-all-start.2 = ((bf16[32,16,128]{2,1,0:T(8,128)(2,1)}), bf16[32,16,128]{2,1,0:T(8,128)(2,1)S(1)}, u32[]{:S(2)}, u32[]{:S(2)}) async-start(bf16[32,16,128]{2,1,0:T(8,128)(2,1)} %broadcast_in_dim.9), calls=%async_computation.2 | async-start | bytes 262144 | tf_op jit(solution)/shard_map/all_to_all | solution.py:91
  130.1 48.5 %all-to-all-start.3 = ((bf16[32,16,128]{2,1,0:T(8,128)(2,1)}), bf16[32,16,128]{2,1,0:T(8,128)(2,1)S(1)}, u32[]{:S(2)}, u32[]{:S(2)}) async-start(bf16[32,16,128]{2,1,0:T(8,128)(2,1)} %bitcast.77), calls=%async_computation.3 | async-start | bytes 262144 | tf_op jit(solution)/shard_map/all_to_all | solution.py:82
  166.0 15.9 %collective-permute-start.8 = (bf16[1536,128]{1,0:T(8,128)(2,1)}, bf16[1536,128]{1,0:T(8,128)(2,1)}, u32[]{:S(2)}, u32[]{:S(2)}) collective-permute-start(bf16[1536,128]{1,0:T(8,128)(2,1)} %fusion.5), channel_id=1, source_target_pairs={{0,32},{32,0},{64,96},{96,64},{128,160},{160,128},{192,224},{224,1... | collective-permute-start | bytes 1179656 | tf_op jit(solution)/shard_map/ppermute | solution.py:99
  178.7 3.2 %collective-permute-start.9 = (bf16[32,128]{1,0:T(8,128)(2,1)S(1)}, bf16[32,128]{1,0:T(8,128)(2,1)S(1)}, u32[]{:S(2)}, u32[]{:S(2)}) collective-permute-start(bf16[32,128]{1,0:T(8,128)(2,1)S(1)} %pad_maximum_fusion.4), channel_id=1, source_target_pairs={{0,32},{32,0},{64,96},{96,64},{128,160},{160,128},{192,224},{224,1... | collective-permute-start | bytes 24584 | tf_op jit(solution)/shard_map/ppermute | solution.py:86
  184.0 22.9 %collective-permute-start.10 = (bf16[96,128]{1,0:T(8,128)(2,1)S(1)}, bf16[96,128]{1,0:T(8,128)(2,1)S(1)}, u32[]{:S(2)}, u32[]{:S(2)}) collective-permute-start(bf16[96,128]{1,0:T(8,128)(2,1)S(1)} %get-tuple-element.13), channel_id=1, source_target_pairs={{0,32},{32,64},{64,96},{96,128},{128,160},{160,192},{192,224},{224... | collective-permute-start | bytes 73736 | tf_op jit(solution)/shard_map/ppermute | solution.py:29
  187.1 24.2 %all-to-all-start.4 = ((bf16[16,32,128]{2,1,0:T(8,128)(2,1)}), bf16[16,32,128]{2,1,0:T(8,128)(2,1)S(1)}, u32[]{:S(2)}, u32[]{:S(2)}) async-start(bf16[16,32,128]{2,1,0:T(8,128)(2,1)} %broadcast_in_dim.10), calls=%async_computation.4 | async-start | bytes 262144 | tf_op jit(solution)/shard_map/all_to_all | solution.py:88
  196.7 12.2 %collective-permute-start.11 = (bf16[96,128]{1,0:T(8,128)(2,1)S(1)}, bf16[96,128]{1,0:T(8,128)(2,1)S(1)}, u32[]{:S(2)}, u32[]{:S(2)}) collective-permute-start(bf16[96,128]{1,0:T(8,128)(2,1)S(1)} %get-tuple-element.12), channel_id=1, source_target_pairs={{32,0},{64,32},{96,64},{128,96},{160,128},{192,160},{224,192},{256... | collective-permute-start | bytes 73736 | tf_op jit(solution)/shard_map/ppermute | solution.py:30
  198.6 10.9 %collective-permute-start.12 = (bf16[96,128]{1,0:T(8,128)(2,1)S(1)}, bf16[96,128]{1,0:T(8,128)(2,1)S(1)}, u32[]{:S(2)}, u32[]{:S(2)}) collective-permute-start(bf16[96,128]{1,0:T(8,128)(2,1)S(1)} %get-tuple-element.11), channel_id=1, source_target_pairs={{0,8},{8,16},{16,24},{1,9},{9,17},{17,25},{2,10},{10,18},{18,26},{... | collective-permute-start | bytes 73736 | tf_op jit(solution)/shard_map/ppermute | solution.py:29
  202.5 7.6 %collective-permute-start.13 = (bf16[96,128]{1,0:T(8,128)(2,1)S(1)}, bf16[96,128]{1,0:T(8,128)(2,1)S(1)}, u32[]{:S(2)}, u32[]{:S(2)}) collective-permute-start(bf16[96,128]{1,0:T(8,128)(2,1)S(1)} %get-tuple-element.10), channel_id=1, source_target_pairs={{8,0},{16,8},{24,16},{9,1},{17,9},{25,17},{10,2},{18,10},{26,18},{... | collective-permute-start | bytes 73736 | tf_op jit(solution)/shard_map/ppermute | solution.py:30
  203.8 6.9 %collective-permute-start.14 = (bf16[96,128]{1,0:T(8,128)(2,1)S(1)}, bf16[96,128]{1,0:T(8,128)(2,1)S(1)}, u32[]{:S(2)}, u32[]{:S(2)}) collective-permute-start(bf16[96,128]{1,0:T(8,128)(2,1)S(1)} %get-tuple-element.9), channel_id=1, source_target_pairs={{0,1},{1,2},{2,3},{3,4},{4,5},{5,6},{6,7},{8,9},{9,10},{10,11},{11... | collective-permute-start | bytes 73736 | tf_op jit(solution)/shard_map/ppermute | solution.py:29
  207.0 16.8 %collective-permute-start.15 = (bf16[96,128]{1,0:T(8,128)(2,1)S(1)}, bf16[96,128]{1,0:T(8,128)(2,1)S(1)}, u32[]{:S(2)}, u32[]{:S(2)}) collective-permute-start(bf16[96,128]{1,0:T(8,128)(2,1)S(1)} %get-tuple-element.8), channel_id=1, source_target_pairs={{1,0},{2,1},{3,2},{4,3},{5,4},{6,5},{7,6},{9,8},{10,9},{11,10},{12... | collective-permute-start | bytes 73736 | tf_op jit(solution)/shard_map/ppermute | solution.py:30
  212.0 20.9 %all-to-all-start.5 = ((bf16[32,16,128]{2,1,0:T(8,128)(2,1)}), bf16[32,16,128]{2,1,0:T(8,128)(2,1)S(1)}, u32[]{:S(2)}, u32[]{:S(2)}) async-start(bf16[32,16,128]{2,1,0:T(8,128)(2,1)} %broadcast_in_dim.11), calls=%async_computation.5 | async-start | bytes 262144 | tf_op jit(solution)/shard_map/all_to_all | solution.py:91
  (9 other events, 76.5 us)

commit v3 on v2

--- a/solution.py
+++ b/solution.py
@@ -66,6 +66,7 @@
     other_core = [(i, i ^ 1) for i in range(n_gx)]
     flat_faces = face_rows[0].reshape(-1)
     select = (flat_faces[:, None] == jnp.arange(loads.shape[1], dtype=jnp.int32)[None, :]).astype(BF16)
+    select = lax.optimization_barrier(select)
     digits = map_rows(coarse_map)
     basis_faces = dot(select, coarse_basis, (1, 1)).astype(BF16)
     root_at_faces = dot(basis_faces, root_coupling, (1, 0)).astype(BF16)
@@ -75,22 +76,44 @@
         number = values[:, 0:2] * RADIX + values[:, 2:4]
         return number.reshape(rows.shape[0], -1)[:, :coarse_dofs].reshape(-1).astype(jnp.int32)
 
+    def swap(blocks, axes):
+        return lax.all_to_all(blocks, axes, 0, 0, tiled=True)
+
+    def reduce_plane(rows, staged):
+        if not staged:
+            pieces = swap(rows.reshape(plane, part, 128), PLANE)
+            return jnp.sum(pieces.astype(F32), axis=0)
+        pieces = swap(rows.reshape(n_gz, n_gy * part, 128), "gz")
+        kept = high_low(jnp.sum(pieces.astype(F32), axis=0).reshape(n_gy, part, 128))
+        pieces = swap(kept, "gy")
+        return jnp.sum(rejoin(pieces), axis=0)
+
+    def spread_plane(rows, staged):
+        if not staged:
+            return swap(jnp.broadcast_to(rows[None], (plane,) + rows.shape), PLANE).reshape(root_dofs, 128)
+        rows = swap(jnp.broadcast_to(rows[None], (n_gy,) + rows.shape), "gy").reshape(-1, 128)
+        return swap(jnp.broadcast_to(rows[None], (n_gz,) + rows.shape), "gz").reshape(root_dofs, 128)
+
     def apply_pre(rounded, selector):
+        staged = selector is not None
         near = dot(rounded, stiff_inverse, (1, 0))
         coarse_t = dot(coarse_basis, rounded, (1, 1)).astype(BF16)
         root_term = dot(root_coupling, coarse_t, (0, 0)).astype(BF16)
-        pieces = lax.all_to_all(root_term.reshape(plane, part, 128), PLANE, 0, 0, tiled=True)
-        parts = [coarse_t] + ([digits] if selector is None else [])
-        everyone = lax.all_gather(jnp.concatenate(parts, axis=0), "gx", axis_index_groups=same_core)
-        mine = jnp.sum(pieces.astype(F32), axis=0)
-        pair = mine + rejoin(lax.ppermute(high_low(mine), "gx", other_core))
-        spread = jnp.broadcast_to(high_low(pair)[None], (n_gx // 2, 2 * part, 128))
-        lines = lax.all_to_all(spread, "gx", 0, 0, axis_index_groups=same_core, tiled=True)
-        root_rows = jnp.sum(rejoin(lines), axis=0)
-        spread = jnp.broadcast_to(root_rows.astype(BF16)[None], (plane, part, 128))
-        root_total = lax.all_to_all(spread, PLANE, 0, 0, tiled=True).reshape(root_dofs, 128)
+        mine = high_low(reduce_plane(root_term, staged))
+        top = coarse_dofs + mine.shape[0]
+        parts = [coarse_t, mine] + ([digits] if selector is None else [])
+        payload = jnp.concatenate(parts, axis=0)
+        if staged:
+            payload = lax.optimization_barrier(payload.reshape(-1, 16, 128))
+            everyone = lax.optimization_barrier(lax.all_gather(payload[None], "gx", axis_index_groups=same_core, axis=0, tiled=True))
+            everyone = everyone.reshape(n_gx // 2, -1, 128)
+        else:
+            everyone = lax.all_gather(payload, "gx", axis_index_groups=same_core)
+        root_half = jnp.sum(rejoin(everyone[:, coarse_dofs:top]), axis=0)
+        root_rows = root_half + rejoin(lax.ppermute(high_low(root_half), "gx", other_core))
+        root_total = spread_plane(root_rows.astype(BF16), staged)
         if selector is None:
-            numbers = gathered_map(everyone[:, coarse_dofs : coarse_dofs + 4])
+            numbers = gathered_map(everyone[:, top : top + 4])
             selector = (
                 jnp.arange(GROUP_DOFS, dtype=jnp.int32)[:, None] == numbers[None, :]
             ).astype(BF16)

time: 243 us -> 238 us (0.979)
  starting transfers between devices: 101 us -> 77.9 us
  blocking collectives: 68.9 us -> 87.1 us
  waiting for transfers between devices: 23.2 us -> 19.9 us
    all_to_all x6 -> x4, starting transfers between devices: 46.3 us -> 21.1 us  [swap(): return lax.all_to_all(blocks, axes, 0, 0, tiled=True)]
    all_to_all x0 -> x2, blocking collectives: none -> 19.5 us  [swap(): return lax.all_to_all(blocks, axes, 0, 0, tiled=True)]
    ppermute x2, starting transfers between devices: 6.16 us -> 23.5 us  [apply_pre(): lax.ppermute(high_low(root_half), 'gx', other_core)]
    ppermute x2, starting transfers between devices: 22.4 us -> 5.3 us  [apply_pre(): other = lax.ppermute(group_half, 'gx', other_core)]
    all_to_all x6 -> x4, waiting for transfers between devices: 22.3 us -> 16.6 us  [swap(): return lax.all_to_all(blocks, axes, 0, 0, tiled=True)]
    ppermute x6, waiting for transfers between devices: 0.02 us -> 2.46 us  [exchange_faces(): received.append(lax.ppermute(faces[2 * d], axis, down))]
    unnamed x33 -> x57, local copies, waits for them, and re-layouts: 7.7 us -> 9.17 us
  transfers between devices with their start and end apart: 22 -> 20, of which waited for: 5 -> 5; matrix products, arithmetic and copies ran while one was open for 9% -> 13% of each run, Pallas kernels for 0% -> 0%
where the time goes in v3:
time: 238 us; the launch traced here: 234 us
  blocking collectives  87.1 us (37%)
  starting transfers between devices  77.9 us (33%)
  matrix products  31.9 us (13%)
  waiting for transfers between devices  19.9 us (8%)
  local copies, waits for them, and re-layouts  14.5 us (6%)
    all_gather x1, blocking collectives, apply_pre(): everyone = lax.all_gather(payload, 'gx', axis_index_groups=same_core)  41.7 us
    dot_general x25, matrix products, dot(): lax.dot_general(a, b, ((dims[0:1], dims[1:2]), ((), ())), preferred_eleme...  31.9 us
    all_gather x1, blocking collectives, apply_pre(): lax.all_gather(payload[None], 'gx', axis_index_groups=same_core, axis=0,...  25.9 us
    ppermute x2, starting transfers between devices, apply_pre(): lax.ppermute(high_low(root_half), 'gx', other_core)  23.5 us
    all_to_all x4, starting transfers between devices, swap(): return lax.all_to_all(blocks, axes, 0, 0, tiled=True)  21.1 us
    all_to_all x2, blocking collectives, swap(): return lax.all_to_all(blocks, axes, 0, 0, tiled=True)  19.5 us
    ppermute x6, starting transfers between devices, exchange_faces(): received.append(lax.ppermute(faces[2 * d + 1], axis, up))  18.2 us
    all_to_all x4, waiting for transfers between devices, swap(): return lax.all_to_all(blocks, axes, 0, 0, tiled=True)  16.6 us
  transfers between devices with their start and end apart: 20, of which 5 were waited for; matrix products, arithmetic and copies ran while one was open for 13% of the time, Pallas kernels for 0%

profile of v3, /device:TPU:1, one launch (start us, length us, event | category | flops | bytes accessed | tf_op | source)
XLA Modules:
  0.0 234.1 jit_solution(2961086869199233437)
XLA Ops:
  4.1 10.5 %all-to-all-start = ((bf16[32,16,128]{2,1,0:T(8,128)(2,1)}), bf16[32,16,128]{2,1,0:T(8,128)(2,1)S(1)}, u32[]{:S(2)}, u32[]{:S(2)}) async-start(bf16[32,16,128]{2,1,0:T(8,128)(2,1)} %bitcast.1), calls=%async_computation | async-start | bytes 262144 | tf_op jit(solution)/shard_map/all_to_all | solution.py:80
  16.4 7.3 %all-to-all-done = bf16[32,16,128]{2,1,0:T(8,128)(2,1)S(1)} async-done(((bf16[32,16,128]{2,1,0:T(8,128)(2,1)}), bf16[32,16,128]{2,1,0:T(8,128)(2,1)S(1)}, u32[]{:S(2)}, u32[]{:S(2)}) %all-to-all-start) | async-done | bytes 131104 | tf_op jit(solution)/shard_map/all_to_all | solution.py:80
  23.8 41.7 %all-gather = bf16[3840,128]{1,0:T(8,128)(2,1)S(1)} all-gather(bf16[240,128]{1,0:T(8,128)(2,1)S(1)} %pad_maximum_fusion.1), channel_id=2, replica_groups={{0,64,128,192,256,320,384,448,512,576,640,704,768,832,896,960},{32,96,1..., dimensions={0}, use_global_device_ids=true | all-gather | bytes 1044480 | tf_op jit(solution)/shard_map/all_gather | solution.py:111
  65.8 10.2 %collective-permute-start.1 = (bf16[32,128]{1,0:T(8,128)(2,1)S(1)}, bf16[32,128]{1,0:T(8,128)(2,1)S(1)}, u32[]{:S(2)}, u32[]{:S(2)}) collective-permute-start(bf16[32,128]{1,0:T(8,128)(2,1)S(1)} %pad_maximum_fusion.4), channel_id=1, source_target_pairs={{0,32},{32,0},{64,96},{96,64},{128,160},{160,128},{192,224},{224,1... | collective-permute-start | bytes 24584 | tf_op jit(solution)/shard_map/ppermute | solution.py:113
  76.0 4.1 %fusion.4 = bf16[1536,128]{1,0:T(8,128)(2,1)} fusion(bf16[3072,128]{1,0:T(8,128)(2,1)S(1)} %bitcast.92, s32[3072]{0:T(1024)S(1)} %convert_element_type.205), kind=kOutput, calls=%fused_computation.5 | convolution fusion | flops 1212874752 | bytes 1191936 | tf_op jit(solution)/shard_map/dot_general | solution.py:15
  82.7 3.9 %all-to-all-start.1 = ((bf16[32,16,128]{2,1,0:T(8,128)(2,1)}), bf16[32,16,128]{2,1,0:T(8,128)(2,1)S(1)}, u32[]{:S(2)}, u32[]{:S(2)}) async-start(bf16[32,16,128]{2,1,0:T(8,128)(2,1)} %broadcast_in_dim.10), calls=%async_computation.1 | async-start | bytes 262144 | tf_op jit(solution)/shard_map/all_to_all | solution.py:80
  87.7 8.1 %all-to-all-done.1 = bf16[32,16,128]{2,1,0:T(8,128)(2,1)S(1)} async-done(((bf16[32,16,128]{2,1,0:T(8,128)(2,1)}), bf16[32,16,128]{2,1,0:T(8,128)(2,1)S(1)}, u32[]{:S(2)}, u32[]{:S(2)}) %all-to-all-start.1) | async-done | bytes 131104 | tf_op jit(solution)/shard_map/all_to_all | solution.py:80
  100.4 3.4 %collective-permute-start.2 = (bf16[96,640]{1,0:T(8,128)(2,1)}, bf16[96,640]{1,0:T(8,128)(2,1)}, u32[]{:S(2)}, u32[]{:S(2)}) collective-permute-start(bf16[96,640]{1,0:T(8,128)(2,1)} %get-tuple-element.3), channel_id=1, source_target_pairs={{0,32},{32,64},{64,96},{96,128},{128,160},{160,192},{192,224},{224... | collective-permute-start | bytes 368648 | tf_op jit(solution)/shard_map/ppermute | solution.py:29
  103.8 2.6 %collective-permute-start.3 = (bf16[96,640]{1,0:T(8,128)(2,1)}, bf16[96,640]{1,0:T(8,128)(2,1)}, u32[]{:S(2)}, u32[]{:S(2)}) collective-permute-start(bf16[96,640]{1,0:T(8,128)(2,1)} %get-tuple-element.4), channel_id=1, source_target_pairs={{32,0},{64,32},{96,64},{128,96},{160,128},{192,160},{224,192},{256... | collective-permute-start | bytes 368648 | tf_op jit(solution)/shard_map/ppermute | solution.py:30
  106.3 2.9 %collective-permute-start.4 = (bf16[96,640]{1,0:T(8,128)(2,1)}, bf16[96,640]{1,0:T(8,128)(2,1)}, u32[]{:S(2)}, u32[]{:S(2)}) collective-permute-start(bf16[96,640]{1,0:T(8,128)(2,1)} %get-tuple-element.5), channel_id=1, source_target_pairs={{0,8},{8,16},{16,24},{1,9},{9,17},{17,25},{2,10},{10,18},{18,26},{... | collective-permute-start | bytes 368648 | tf_op jit(solution)/shard_map/ppermute | solution.py:29
  110.5 3.5 %collective-permute-start.6 = (bf16[96,640]{1,0:T(8,128)(2,1)S(1)}, bf16[96,640]{1,0:T(8,128)(2,1)}, u32[]{:S(2)}, u32[]{:S(2)}) collective-permute-start(bf16[96,640]{1,0:T(8,128)(2,1)S(1)} %get-tuple-element.7), channel_id=1, source_target_pairs={{0,1},{1,2},{2,3},{3,4},{4,5},{5,6},{6,7},{8,9},{9,10},{10,11},{11... | collective-permute-start | bytes 368648 | tf_op jit(solution)/shard_map/ppermute | solution.py:29
  124.3 2.6 %fusion.11 = f32[128,640]{1,0:T(8,128)} fusion(bf16[576,640]{1,0:T(8,128)(2,1)S(1)} %fusion.6, bf16[128,512]{1,0:T(8,128)(2,1)S(1)} %convolution_convert_fusion.7, bf16[576,640]{1,0:T(8,128)(2,1)} %constant_dynamic-update-slice_fusion), kind=kOutput, calls=%fused_computation.34 | convolution fusion | flops 169943040 | bytes 1785856 | tf_op jit(solution)/shard_map/dot_general | solution.py:15
  129.2 12.1 %all_to_all.30 = bf16[8,64,128]{2,1,0:T(8,128)(2,1)S(1)} all-to-all(bf16[8,64,128]{2,1,0:T(8,128)(2,1)S(1)} %bitcast.94), channel_id=1, replica_groups=mesh['gx'=32,'gy'=4,'gz'=8] {'gz'}, dimensions={0} | all-to-all | bytes 262144 | tf_op jit(solution)/shard_map/all_to_all | solution.py:80
  141.3 7.5 %all_to_all.31 = bf16[4,32,128]{2,1,0:T(8,128)(2,1)S(1)} all-to-all(bf16[4,32,128]{2,1,0:T(8,128)(2,1)S(1)} %pad_maximum_fusion.3), channel_id=1, replica_groups=mesh['gx'=32,'gy'=4,'gz'=8] {'gy'}, dimensions={0} | all-to-all | bytes 65536 | tf_op jit(solution)/shard_map/all_to_all | solution.py:80
  148.8 25.9 %all-gather.1 = bf16[224,16,128]{2,1,0:T(8,128)(2,1)S(1)} all-gather(bf16[14,16,128]{2,1,0:T(8,128)(2,1)S(1)} %bitcast.98), channel_id=3, replica_groups={{0,64,128,192,256,320,384,448,512,576,640,704,768,832,896,960},{32,96,1..., dimensions={0}, use_global_device_ids=true | all-gather | bytes 974848 | tf_op jit(solution)/shard_map/all_gather | solution.py:108
  174.8 13.3 %collective-permute-start.9 = (bf16[32,128]{1,0:T(8,128)(2,1)S(1)}, bf16[32,128]{1,0:T(8,128)(2,1)S(1)}, u32[]{:S(2)}, u32[]{:S(2)}) collective-permute-start(bf16[32,128]{1,0:T(8,128)(2,1)S(1)} %pad_maximum_fusion.5), channel_id=1, source_target_pairs={{0,32},{32,0},{64,96},{96,64},{128,160},{160,128},{192,224},{224,1... | collective-permute-start | bytes 24584 | tf_op jit(solution)/shard_map/ppermute | solution.py:113
  189.5 3.2 %all-to-all-start.4 = ((bf16[4,16,128]{2,1,0:T(8,128)(2,1)}), bf16[4,16,128]{2,1,0:T(8,128)(2,1)S(1)}, u32[]{:S(2)}, u32[]{:S(2)}) async-start(bf16[4,16,128]{2,1,0:T(8,128)(2,1)} %broadcast_in_dim.12), calls=%async_computation.4 | async-start | bytes 32768 | tf_op jit(solution)/shard_map/all_to_all | solution.py:80
  197.6 3.5 %all-to-all-start.5 = ((bf16[8,64,128]{2,1,0:T(8,128)(2,1)}), bf16[8,64,128]{2,1,0:T(8,128)(2,1)S(1)}, u32[]{:S(2)}, u32[]{:S(2)}) async-start(bf16[8,64,128]{2,1,0:T(8,128)(2,1)} %broadcast_in_dim.14), calls=%async_computation.5 | async-start | bytes 262144 | tf_op jit(solution)/shard_map/all_to_all | solution.py:80
  201.2 5.3 %fusion.5 = bf16[1536,128]{1,0:T(8,128)(2,1)} fusion(bf16[3072,128]{1,0:T(8,128)(2,1)} %bitcast.93, s32[3072]{0:T(1024)S(1)} %convert_element_type.205), kind=kOutput, calls=%fused_computation.6 | convolution fusion | flops 1212874752 | bytes 1191936 | tf_op jit(solution)/shard_map/dot_general | solution.py:15
  206.5 3.4 %collective-permute-start.8 = (bf16[1536,128]{1,0:T(8,128)(2,1)}, bf16[1536,128]{1,0:T(8,128)(2,1)}, u32[]{:S(2)}, u32[]{:S(2)}) collective-permute-start(bf16[1536,128]{1,0:T(8,128)(2,1)} %fusion.5), channel_id=1, source_target_pairs={{0,32},{32,0},{64,96},{96,64},{128,160},{160,128},{192,224},{224,1... | collective-permute-start | bytes 1179656 | tf_op jit(solution)/shard_map/ppermute | solution.py:122
  210.2 2.7 %fusion.12 = f32[128,640]{1,0:T(8,128)} fusion(bf16[576,640]{1,0:T(8,128)(2,1)S(1)} %fusion.6, bf16[576,640]{1,0:T(8,128)(2,1)} %constant_dynamic-update-slice_fusion, bf16[128,512]{1,0:T(8,128)(2,1)S(1)} %convolution_convert_fusion.6, bf16[128,512]{1,0:T(8,128)(2,1)S(1)} %convolution_convert_fusion.7), kind=kOutput, calls=%fused_computation.35 | convolution fusion | flops 170205184 | bytes 1916928 | tf_op jit(solution)/shard_map/dot_general | solution.py:15
  215.6 3.4 %collective-permute-start.10 = (bf16[96,128]{1,0:T(8,128)(2,1)}, bf16[96,128]{1,0:T(8,128)(2,1)}, u32[]{:S(2)}, u32[]{:S(2)}) collective-permute-start(bf16[96,128]{1,0:T(8,128)(2,1)} %get-tuple-element.13), channel_id=1, source_target_pairs={{0,32},{32,64},{64,96},{96,128},{128,160},{160,192},{192,224},{224... | collective-permute-start | bytes 73736 | tf_op jit(solution)/shard_map/ppermute | solution.py:29
  225.2 2.9 %collective-permute-start.14 = (bf16[96,128]{1,0:T(8,128)(2,1)S(1)}, bf16[96,128]{1,0:T(8,128)(2,1)S(1)}, u32[]{:S(2)}, u32[]{:S(2)}) collective-permute-start(bf16[96,128]{1,0:T(8,128)(2,1)S(1)} %get-tuple-element.9), channel_id=1, source_target_pairs={{0,1},{1,2},{2,3},{3,4},{4,5},{5,6},{6,7},{8,9},{9,10},{10,11},{11... | collective-permute-start | bytes 73736 | tf_op jit(solution)/shard_map/ppermute | solution.py:29
  230.3 2.4 %collective-permute-done.15 = bf16[96,128]{1,0:T(8,128)(2,1)S(1)} collective-permute-done((bf16[96,128]{1,0:T(8,128)(2,1)S(1)}, bf16[96,128]{1,0:T(8,128)(2,1)S(1)}, u32[]{:S(2)}, u32[]{:S(2)}) %collective-permute-start.15) | collective-permute-done | bytes 24608 | tf_op jit(solution)/shard_map/ppermute | solution.py:30
  (144 shorter events, 46.4 us)
Async XLA Ops:
  0.6 86.0 %copy-start = (bf16[640,640]{1,0:T(8,128)(2,1)S(1)}, bf16[640,640]{1,0:T(8,128)(2,1)}, u32[]{:S(2)}) copy-start(bf16[640,640]{1,0:T(8,128)(2,1)} %param.11) | copy-start | bytes 2457604
  0.7 13.9 %copy-start.21 = (s32[1,6,96]{2,0,1:T(1,128)S(1)}, s32[1,6,96]{2,0,1:T(1,128)}, u32[]{:S(2)}) copy-start(s32[1,6,96]{2,0,1:T(1,128)} %param.12) | copy-start | bytes 6916
  4.1 19.6 %all-to-all-start = ((bf16[32,16,128]{2,1,0:T(8,128)(2,1)}), bf16[32,16,128]{2,1,0:T(8,128)(2,1)S(1)}, u32[]{:S(2)}, u32[]{:S(2)}) async-start(bf16[32,16,128]{2,1,0:T(8,128)(2,1)} %bitcast.1), calls=%async_computation | async-start | bytes 262144 | tf_op jit(solution)/shard_map/all_to_all | solution.py:80
  65.8 16.2 %collective-permute-start.1 = (bf16[32,128]{1,0:T(8,128)(2,1)S(1)}, bf16[32,128]{1,0:T(8,128)(2,1)S(1)}, u32[]{:S(2)}, u32[]{:S(2)}) collective-permute-start(bf16[32,128]{1,0:T(8,128)(2,1)S(1)} %pad_maximum_fusion.4), channel_id=1, source_target_pairs={{0,32},{32,0},{64,96},{96,64},{128,160},{160,128},{192,224},{224,1... | collective-permute-start | bytes 24584 | tf_op jit(solution)/shard_map/ppermute | solution.py:113
  80.1 17.0 %collective-permute-start = (bf16[1536,128]{1,0:T(8,128)(2,1)}, bf16[1536,128]{1,0:T(8,128)(2,1)}, u32[]{:S(2)}, u32[]{:S(2)}) collective-permute-start(bf16[1536,128]{1,0:T(8,128)(2,1)} %fusion.4), channel_id=1, source_target_pairs={{0,32},{32,0},{64,96},{96,64},{128,160},{160,128},{192,224},{224,1... | collective-permute-start | bytes 1179656 | tf_op jit(solution)/shard_map/ppermute | solution.py:122
  82.7 13.0 %all-to-all-start.1 = ((bf16[32,16,128]{2,1,0:T(8,128)(2,1)}), bf16[32,16,128]{2,1,0:T(8,128)(2,1)S(1)}, u32[]{:S(2)}, u32[]{:S(2)}) async-start(bf16[32,16,128]{2,1,0:T(8,128)(2,1)} %broadcast_in_dim.10), calls=%async_computation.1 | async-start | bytes 262144 | tf_op jit(solution)/shard_map/all_to_all | solution.py:80
  100.4 14.1 %collective-permute-start.2 = (bf16[96,640]{1,0:T(8,128)(2,1)}, bf16[96,640]{1,0:T(8,128)(2,1)}, u32[]{:S(2)}, u32[]{:S(2)}) collective-permute-start(bf16[96,640]{1,0:T(8,128)(2,1)} %get-tuple-element.3), channel_id=1, source_target_pairs={{0,32},{32,64},{64,96},{96,128},{128,160},{160,192},{192,224},{224... | collective-permute-start | bytes 368648 | tf_op jit(solution)/shard_map/ppermute | solution.py:29
  103.8 13.6 %collective-permute-start.3 = (bf16[96,640]{1,0:T(8,128)(2,1)}, bf16[96,640]{1,0:T(8,128)(2,1)}, u32[]{:S(2)}, u32[]{:S(2)}) collective-permute-start(bf16[96,640]{1,0:T(8,128)(2,1)} %get-tuple-element.4), channel_id=1, source_target_pairs={{32,0},{64,32},{96,64},{128,96},{160,128},{192,160},{224,192},{256... | collective-permute-start | bytes 368648 | tf_op jit(solution)/shard_map/ppermute | solution.py:30
  106.3 12.6 %collective-permute-start.4 = (bf16[96,640]{1,0:T(8,128)(2,1)}, bf16[96,640]{1,0:T(8,128)(2,1)}, u32[]{:S(2)}, u32[]{:S(2)}) collective-permute-start(bf16[96,640]{1,0:T(8,128)(2,1)} %get-tuple-element.5), channel_id=1, source_target_pairs={{0,8},{8,16},{16,24},{1,9},{9,17},{17,25},{2,10},{10,18},{18,26},{... | collective-permute-start | bytes 368648 | tf_op jit(solution)/shard_map/ppermute | solution.py:29
  109.2 11.3 %collective-permute-start.5 = (bf16[96,640]{1,0:T(8,128)(2,1)S(1)}, bf16[96,640]{1,0:T(8,128)(2,1)}, u32[]{:S(2)}, u32[]{:S(2)}) collective-permute-start(bf16[96,640]{1,0:T(8,128)(2,1)S(1)} %get-tuple-element.6), channel_id=1, source_target_pairs={{8,0},{16,8},{24,16},{9,1},{17,9},{25,17},{10,2},{18,10},{26,18},{... | collective-permute-start | bytes 368648 | tf_op jit(solution)/shard_map/ppermute | solution.py:30
  110.5 11.6 %collective-permute-start.6 = (bf16[96,640]{1,0:T(8,128)(2,1)S(1)}, bf16[96,640]{1,0:T(8,128)(2,1)}, u32[]{:S(2)}, u32[]{:S(2)}) collective-permute-start(bf16[96,640]{1,0:T(8,128)(2,1)S(1)} %get-tuple-element.7), channel_id=1, source_target_pairs={{0,1},{1,2},{2,3},{3,4},{4,5},{5,6},{6,7},{8,9},{9,10},{10,11},{11... | collective-permute-start | bytes 368648 | tf_op jit(solution)/shard_map/ppermute | solution.py:29
  114.5 9.1 %collective-permute-start.7 = (bf16[96,640]{1,0:T(8,128)(2,1)S(1)}, bf16[96,640]{1,0:T(8,128)(2,1)S(1)}, u32[]{:S(2)}, u32[]{:S(2)}) collective-permute-start(bf16[96,640]{1,0:T(8,128)(2,1)S(1)} %get-tuple-element.2), channel_id=1, source_target_pairs={{1,0},{2,1},{3,2},{4,3},{5,4},{6,5},{7,6},{9,8},{10,9},{11,10},{12... | collective-permute-start | bytes 368648 | tf_op jit(solution)/shard_map/ppermute | solution.py:30
  128.6 20.2 %copy-start.12 = (bf16[128,640]{1,0:T(8,128)(2,1)}, bf16[128,640]{1,0:T(8,128)(2,1)S(1)}, u32[]{:S(2)}) copy-start(bf16[128,640]{1,0:T(8,128)(2,1)S(1)} %fusion.10) | copy-start | bytes 491524
  174.8 14.1 %collective-permute-start.9 = (bf16[32,128]{1,0:T(8,128)(2,1)S(1)}, bf16[32,128]{1,0:T(8,128)(2,1)S(1)}, u32[]{:S(2)}, u32[]{:S(2)}) collective-permute-start(bf16[32,128]{1,0:T(8,128)(2,1)S(1)} %pad_maximum_fusion.5), channel_id=1, source_target_pairs={{0,32},{32,0},{64,96},{96,64},{128,160},{160,128},{192,224},{224,1... | collective-permute-start | bytes 24584 | tf_op jit(solution)/shard_map/ppermute | solution.py:113
  189.5 7.4 %all-to-all-start.4 = ((bf16[4,16,128]{2,1,0:T(8,128)(2,1)}), bf16[4,16,128]{2,1,0:T(8,128)(2,1)S(1)}, u32[]{:S(2)}, u32[]{:S(2)}) async-start(bf16[4,16,128]{2,1,0:T(8,128)(2,1)} %broadcast_in_dim.12), calls=%async_computation.4 | async-start | bytes 32768 | tf_op jit(solution)/shard_map/all_to_all | solution.py:80
  197.6 12.3 %all-to-all-start.5 = ((bf16[8,64,128]{2,1,0:T(8,128)(2,1)}), bf16[8,64,128]{2,1,0:T(8,128)(2,1)S(1)}, u32[]{:S(2)}, u32[]{:S(2)}) async-start(bf16[8,64,128]{2,1,0:T(8,128)(2,1)} %broadcast_in_dim.14), calls=%async_computation.5 | async-start | bytes 262144 | tf_op jit(solution)/shard_map/all_to_all | solution.py:80
  206.5 6.4 %collective-permute-start.8 = (bf16[1536,128]{1,0:T(8,128)(2,1)}, bf16[1536,128]{1,0:T(8,128)(2,1)}, u32[]{:S(2)}, u32[]{:S(2)}) collective-permute-start(bf16[1536,128]{1,0:T(8,128)(2,1)} %fusion.5), channel_id=1, source_target_pairs={{0,32},{32,0},{64,96},{96,64},{128,160},{160,128},{192,224},{224,1... | collective-permute-start | bytes 1179656 | tf_op jit(solution)/shard_map/ppermute | solution.py:122
  215.6 12.5 %collective-permute-start.10 = (bf16[96,128]{1,0:T(8,128)(2,1)}, bf16[96,128]{1,0:T(8,128)(2,1)}, u32[]{:S(2)}, u32[]{:S(2)}) collective-permute-start(bf16[96,128]{1,0:T(8,128)(2,1)} %get-tuple-element.13), channel_id=1, source_target_pairs={{0,32},{32,64},{64,96},{96,128},{128,160},{160,192},{192,224},{224... | collective-permute-start | bytes 73736 | tf_op jit(solution)/shard_map/ppermute | solution.py:29
  219.6 14.5 %copy-start.14 = (f32[128,640]{1,0:T(8,128)}, f32[128,640]{1,0:T(8,128)S(1)}, u32[]{:S(2)}) copy-start(f32[128,640]{1,0:T(8,128)S(1)} %fusion.7) | copy-start | bytes 983044
  219.6 10.5 %collective-permute-start.11 = (bf16[96,128]{1,0:T(8,128)(2,1)}, bf16[96,128]{1,0:T(8,128)(2,1)S(1)}, u32[]{:S(2)}, u32[]{:S(2)}) collective-permute-start(bf16[96,128]{1,0:T(8,128)(2,1)} %get-tuple-element.12), channel_id=1, source_target_pairs={{32,0},{64,32},{96,64},{128,96},{160,128},{192,160},{224,192},{256... | collective-permute-start | bytes 73736 | tf_op jit(solution)/shard_map/ppermute | solution.py:30
  221.7 8.5 %collective-permute-start.12 = (bf16[96,128]{1,0:T(8,128)(2,1)S(1)}, bf16[96,128]{1,0:T(8,128)(2,1)S(1)}, u32[]{:S(2)}, u32[]{:S(2)}) collective-permute-start(bf16[96,128]{1,0:T(8,128)(2,1)S(1)} %get-tuple-element.11), channel_id=1, source_target_pairs={{0,8},{8,16},{16,24},{1,9},{9,17},{17,25},{2,10},{10,18},{18,26},{... | collective-permute-start | bytes 73736 | tf_op jit(solution)/shard_map/ppermute | solution.py:29
  223.9 6.3 %collective-permute-start.13 = (bf16[96,128]{1,0:T(8,128)(2,1)S(1)}, bf16[96,128]{1,0:T(8,128)(2,1)S(1)}, u32[]{:S(2)}, u32[]{:S(2)}) collective-permute-start(bf16[96,128]{1,0:T(8,128)(2,1)S(1)} %get-tuple-element.10), channel_id=1, source_target_pairs={{8,0},{16,8},{24,16},{9,1},{17,9},{25,17},{10,2},{18,10},{26,18},{... | collective-permute-start | bytes 73736 | tf_op jit(solution)/shard_map/ppermute | solution.py:30
  225.2 5.0 %collective-permute-start.14 = (bf16[96,128]{1,0:T(8,128)(2,1)S(1)}, bf16[96,128]{1,0:T(8,128)(2,1)S(1)}, u32[]{:S(2)}, u32[]{:S(2)}) collective-permute-start(bf16[96,128]{1,0:T(8,128)(2,1)S(1)} %get-tuple-element.9), channel_id=1, source_target_pairs={{0,1},{1,2},{2,3},{3,4},{4,5},{5,6},{6,7},{8,9},{9,10},{10,11},{11... | collective-permute-start | bytes 73736 | tf_op jit(solution)/shard_map/ppermute | solution.py:29
  228.1 4.6 %collective-permute-start.15 = (bf16[96,128]{1,0:T(8,128)(2,1)S(1)}, bf16[96,128]{1,0:T(8,128)(2,1)S(1)}, u32[]{:S(2)}, u32[]{:S(2)}) collective-permute-start(bf16[96,128]{1,0:T(8,128)(2,1)S(1)} %get-tuple-element.8), channel_id=1, source_target_pairs={{1,0},{2,1},{3,2},{4,3},{5,4},{6,5},{7,6},{9,8},{10,9},{11,10},{12... | collective-permute-start | bytes 73736 | tf_op jit(solution)/shard_map/ppermute | solution.py:30
  (19 other events, 138.4 us)
